TPU v7x, 256 devices: a whole 4x4x8 slice. The times are simulated.
256 devices in a mesh: dp: 64 (over x, z_lo, y), pipe: 4 (over z_hi, core).
Axes of the slice: x: 4, y: 4, z: 8 (z_hi: 2, z_lo: 4; z = z_hi * 4 + z_lo), core: 2. Of those that a mesh axis runs over, the one named last changes fastest.
Arguments:
- hidden: bfloat16 [16384, 2048], P('dp'), may hold values from -16 to 16
- gain: float32 [2048], replicated, may hold values from 0.25 to 1.75
- w_value: bfloat16 [4, 2048, 2048], P('pipe', 'dp'), may hold values from -0.125 to 0.125
- d_value: bfloat16 [4, 16384, 2048], P('pipe', 'dp'), may hold values from -3 to 3
Outputs:
- grad_hidden: bfloat16 [16384, 2048], P('dp')
- grad_gain: float32 [2048], P('dp')
- grad_value: float32 [4, 2048, 2048], P('pipe', 'dp')
All inputs are finite; a program needn't handle non-finite values.
Results may differ from a plain program's by a relative error of at most 0.0029.
Values may be sent and summed in bfloat16 or wider, within the bound.
No kernel may reach another device: no remote copies, remote signals or barrier semaphores. Data moves between devices by JAX's collectives and lax.ppermute only.
A program may use at most 64 MiB of HBM per device.

v0:
```python
import jax
import jax.numpy as jnp
from jax import lax
from jax.sharding import PartitionSpec as P

epsilon = 1e-06


def norm_backward(grad_rows, normed_rows, scale_rows, gain):
    scaled = gain * grad_rows
    result = (
        scaled - normed_rows * jnp.mean(scaled * normed_rows, axis=-1, keepdims=True)
    ) / scale_rows
    return (result.astype(jnp.bfloat16), jnp.sum(grad_rows * normed_rows, axis=0))


def weight_term(encoded, operand):
    return lax.dot_general(
        encoded, operand, (((0,), (0,)), ((), ())), preferred_element_type=jnp.float32
    )


def local(hidden, gain, w_value, d_value):
    hidden_f = hidden.astype(jnp.float32)
    row_scale = jnp.sqrt(jnp.mean(hidden_f * hidden_f, axis=-1, keepdims=True) + epsilon)
    normed = hidden_f / row_scale
    encoded = (normed * gain).astype(jnp.bfloat16)
    cotangent = d_value[0]
    projection = w_value[0]
    average = 1.0 / lax.axis_size("dp")
    partial_value = lax.dot_general(
        cotangent,
        lax.all_gather(projection, "dp", axis=0, tiled=True),
        (((1,), (1,)), ((), ())),
        preferred_element_type=jnp.float32,
    )
    grad_encoded = lax.psum(partial_value, "pipe")
    grad_hidden, gain_part = norm_backward(grad_encoded, normed, row_scale, gain)
    gain_share = lax.psum_scatter(gain_part, "dp", scatter_dimension=0, tiled=True)
    grad_gain = gain_share * average
    value_grad = (
        lax.psum_scatter(weight_term(encoded, cotangent), "dp", scatter_dimension=0, tiled=True)
        * average
    )
    return (grad_hidden, grad_gain, value_grad[None])


def solution(mesh):
    return jax.shard_map(
        local,
        mesh=mesh,
        in_specs=(P("dp", None), P(), P("pipe", "dp", None), P("pipe", "dp", None)),
        out_specs=(P("dp", None), P("dp"), P("pipe", "dp", None)),
        check_vma=False,
    )
```

profile of v0, /device:TPU:0, one launch (start us, length us, event | category | flops | bytes accessed | tf_op | source)
XLA Modules:
  0.0 898.9 jit_solution(13786770550400615789)
XLA Ops:
  7.2 0.0 copy-start
  7.2 0.0 all-gather.3.cloned.1.call-start
  7.2 0.7 all-gather.3.cloned.1.call-update
  7.9 0.0 all-reduce.3.cloned.1.call-start
  8.0 363.1 %all-gather.3.cloned.1.call-done = bf16[1,2048,2048]{2,1,0:T(8,128)(2,1)} async-done(((bf16[1,32,2048]{2,1,0:T(8,128)(2,1)}), bf16[1,2048,2048]{2,1,0:T(8,128)(2,1)}) %all-gather.3.cloned.1.call-update) | async-done | bytes 8388624 | tf_op jit(solution)/shard_map/all_gather | solution.py:33
  371.1 0.0 copy-done
  371.1 7.1 fusion
  378.2 0.0 copy-start.1
  378.2 0.0 copy-start.2
  378.2 0.0 all-reduce.3.cloned.1.call-update
  378.2 0.0 reduce-scatter.2.cloned.1.call-start
  378.3 1.1 copy-done.1
  379.4 0.3 fusion.2
  379.7 0.0 copy-done.2
  379.7 8.4 fusion.3
  388.1 0.0 copy-start.3
  388.1 0.0 reduce-scatter.2.cloned.1.call-update
  388.1 0.7 copy-done.3
  388.8 0.6 dynamic-slice
  390.0 87.9 %all-reduce.3.cloned.1.call-done = f32[256,2048]{1,0:T(8,128)} async-done(((f32[256,2048]{1,0:T(8,128)}), f32[256,2048]{1,0:T(8,128)}) %all-reduce.3.cloned.1.call-update) | async-done | bytes 2097168 | tf_op jit(solution)/shard_map/psum | solution.py:37
  478.0 2.2 multiply_reduce_fusion
  480.2 187.4 %all-reduce = f32[2048]{0:T(1024)S(1)} all-reduce(f32[2048]{0:T(1024)S(1)} %get-tuple-element.3), channel_id=3, replica_groups=mesh['dp'=64,'pipe'=4] {'dp'}, use_global_device_ids=true, to_apply=%region_4.0.clone | all-reduce | flops 2048 | bytes 16384
  667.6 0.6 dynamic-slice_multiply_fusion
  668.2 3.1 divide_convert_fusion
  671.3 219.4 %reduce-scatter.2.cloned.1.call-done = f32[32,2048]{1,0:T(8,128)} async-done(((f32[2048,2048]{1,0:T(8,128)}), f32[32,2048]{1,0:T(8,128)}) %reduce-scatter.2.cloned.1.call-update) | async-done | bytes 262160 | tf_op jit(solution)/shard_map/reduce_scatter | solution.py:42
  890.7 1.7 multiply_bitcast_fusion
  (2 shorter events, 0.0 us)
Async XLA Ops:
  7.2 363.9 %copy-start = (bf16[1,256,2048]{2,1,0:T(8,128)(2,1)S(1)}, bf16[1,256,2048]{2,1,0:T(8,128)(2,1)}, u32[]{:S(2)}) copy-start(bf16[1,256,2048]{2,1,0:T(8,128)(2,1)} %param.7) | copy-start | bytes 3145732
  7.2 363.9 %all-gather.3.cloned.1.call-start = ((), (), s32[]{:S(2)}) async-start(), calls=%async_computation.3 | async-start | bytes 8519680 | tf_op jit(solution)/shard_map/all_gather | solution.py:33
  7.9 470.0 %all-reduce.3.cloned.1.call-start = ((), (), s32[]{:S(2)}) async-start(), calls=%async_computation.1 | async-start | bytes 4194304 | tf_op jit(solution)/shard_map/psum | solution.py:37
  378.2 1.2 copy-start.1
  378.2 1.5 copy-start.2
  378.2 512.4 %reduce-scatter.2.cloned.1.call-start = ((), (), s32[]{:S(2)}) async-start(), calls=%async_computation.2 | async-start | bytes 17039360 | tf_op jit(solution)/shard_map/reduce_scatter | solution.py:42
  388.1 0.7 copy-start.3
Sparse Core Ops, SparseCore 0:
  9.8 361.2 all-gather.2
  378.3 99.5 all-reduce.2
  480.5 410.0 reduce-scatter.1
where the time goes:
time: 899 us
  waiting for transfers between devices  671 us (75%)
  blocking collectives  187 us (21%)
  matrix products  15.5 us (2%)
  between operations  14.4 us (2%)
    all_gather x1, waiting for transfers between devices, local(): lax.all_gather(projection, 'dp', axis=0, tiled=True)  363 us
    reduce_scatter x1, waiting for transfers between devices, local(): lax.psum_scatter(weight_term(encoded, cotangent), 'dp', scatter_dimension...  219 us
    unnamed x1, blocking collectives  187 us
    psum x1, waiting for transfers between devices, local(): grad_encoded = lax.psum(partial_value, 'pipe')  87.9 us
  transfers between devices with their start and end apart: 3, of which 3 were waited for; matrix products, arithmetic and copies ran while one was open for 2% of the time, Pallas kernels for 0%

commit v1 on v0

v1 whole, which is shorter than its diff:
```python
import jax
import jax.numpy as jnp
from jax import lax
from jax.experimental import pallas as pl
from jax.experimental.pallas import tpu as pltpu
from jax.sharding import PartitionSpec as P

epsilon = 1e-06
F32, BF16 = jnp.float32, jnp.bfloat16
AXES = ("dp", "pipe")
VMEM = pl.BlockSpec(memory_space=pltpu.VMEM)
SMEM = pl.BlockSpec(memory_space=pltpu.SMEM)


def pairs(dx=0, dy=0, dl=0, dh=0, dc=0):
    out = []
    for x in range(4):
        for zl in range(4):
            for y in range(4):
                for zh in range(2):
                    for c in range(2):
                        source = (((x * 4 + zl) * 4 + y) * 2 + zh) * 2 + c
                        target = ((((x + dx) % 4 * 4 + (zl + dl) % 4) * 4 + (y + dy) % 4) * 2 + (zh + dh) % 2) * 2 + (c + dc) % 2
                        out.append((source, target))
    return out


def send(value, **shift):
    return lax.ppermute(value, AXES, pairs(**shift))


def call(body, outs, flops, *args, scratch=()):
    shapes = [jax.ShapeDtypeStruct(s, t) for s, t in outs]
    moved = sum(v.size * v.dtype.itemsize for v in args) + sum(v.size * v.dtype.itemsize for v in shapes)
    return pl.pallas_call(
        body,
        out_shape=shapes,
        in_specs=[SMEM] + [VMEM] * (len(args) - 1),
        out_specs=[VMEM] * len(shapes),
        scratch_shapes=list(scratch),
        cost_estimate=pl.CostEstimate(flops=flops, bytes_accessed=moved, transcendentals=0),
        compiler_params=pltpu.CompilerParams(vmem_limit_bytes=40 * 1024 * 1024),
    )(*args)


def at(start, size, multiple):
    return pl.ds(pl.multiple_of(start, multiple), size)


def norm_kernel(idx, h, gain, own, p1, p2, p3, scale):
    x, c = idx[0], idx[4]
    h_all = h[...].astype(F32)
    scale[...] = jnp.broadcast_to(jnp.sqrt(jnp.mean(h_all * h_all, axis=-1, keepdims=True) + epsilon), (256, 128))
    columns = at(x * 512, 512, 512)
    own[...] = (h[:, columns].astype(F32) / scale[:, :1] * gain[:, columns]).astype(BF16)
    rows = at(c * 128, 128, 128)
    for k, out in ((1, p1), (2, p2), (3, p3)):
        columns = at((x + k) % 4 * 512, 512, 512)
        out[...] = (h[rows, columns].astype(F32) / scale[rows, :1] * gain[:, columns]).astype(BF16)


def value_kernel(idx, e_own, m1, m2, m3, oth, d0, d1, l0, l1, fa, fb, r0, r1, own, s1, s2, s3, tmp):
    y, c = idx[1], idx[4]

    def dot(a, b):
        return lax.dot_general(a, b, (((0,), (0,)), ((), ())), preferred_element_type=F32)

    def column(j, carry):
        columns = at(j * 256, 256, 256)
        acc = dot(e_own[:128], d0[:, columns]) + dot(e_own[128:], d1[:, columns])
        for k, lo, hi, mine in ((0, l0, l1, m1), (1, fa, fb, m2), (2, r0, r1, m3)):
            first = jnp.where(c == 0, lo[:, columns], hi[:, columns])
            second = jnp.where(c == 0, hi[:, columns], lo[:, columns])
            acc = acc + dot(mine[...], first) + dot(oth[k], second)
        tmp[...] = acc
        for zl in range(4):
            rows = pl.ds(zl * 32, 32)
            own[rows, columns] = tmp[at(zl * 128 + y * 32, 32, 32), :]
            for k, out in ((1, s1), (2, s2), (3, s3)):
                out[rows, columns] = tmp[at(zl * 128 + (y + k) % 4 * 32, 32, 32), :].astype(BF16)
        return carry

    lax.fori_loop(0, 8, column, 0)


def encoded_grad_kernel(idx, w0, w1, w2, w3, d0, d1, l0, l1, fa, fb, r0, r1, keep, give, w):
    y, zl, c = idx[1], idx[2], idx[4]
    for k, block in enumerate((w0, w1, w2, w3)):
        jy = (y + 4 - k) % 4
        for r in range(4):
            jz = (zl + 4 - r) % 4
            w[at((jz * 4 + jy) * 32, 32, 32), :] = block[r * 32 : (r + 1) * 32, :]

    def column(j, carry):
        rows = at(j * 256, 256, 256)
        columns = at(j * 256, 256, 256)
        part = w[rows, :]
        for k, (lo, hi) in enumerate(((d0, d1), (l0, l1), (fa, fb), (r0, r1))):
            p_lo = lax.dot_general(lo[...], part, (((1,), (1,)), ((), ())), preferred_element_type=F32)
            p_hi = lax.dot_general(hi[...], part, (((1,), (1,)), ((), ())), preferred_element_type=F32)
            keep[k, :, columns] = jnp.where(c == 0, p_lo, p_hi)
            give[k, :, columns] = jnp.where(c == 0, p_hi, p_lo)
        return carry

    lax.fori_loop(0, 2, column, 0)


def core_sum_kernel(idx, keep, got, own, give):
    zh = idx[3]
    mine, theirs = at(zh * 64, 64, 64), at((1 - zh) * 64, 64, 64)
    for k in range(4):
        own[k] = keep[k, mine, :] + got[k, mine, :]
        give[k] = (keep[k, theirs, :] + got[k, theirs, :]).astype(BF16)


def half_sum_kernel(idx, own, got, t0, t1, t2, t3):
    for k, out in enumerate((t0, t1, t2, t3)):
        out[...] = own[k] + got[k].astype(F32)


def norm_backward_kernel(idx, h, gain, t0, t1, t2, t3, out):
    x, zh, c = idx[0], idx[3], idx[4]
    rows = at(c * 128 + zh * 64, 64, 64)
    h_all = h[rows, :].astype(F32)
    scale = jnp.sqrt(jnp.mean(h_all * h_all, axis=-1, keepdims=True) + epsilon)
    normed, scaled, total = [], [], 0.0
    for k, term in enumerate((t0, t1, t2, t3)):
        columns = at((x + k) % 4 * 512, 512, 512)
        normed.append(h[rows, columns].astype(F32) / scale)
        scaled.append(gain[:, columns] * term[...])
        total = total + jnp.sum(scaled[k] * normed[k], axis=-1, keepdims=True)
    mean = total / 2048
    for k in range(4):
        columns = at((x + k) % 4 * 512, 512, 512)
        out[:, columns] = ((scaled[k] - normed[k] * mean) / scale).astype(BF16)


def y_sum_kernel(idx, own, g1, g2, g3, w, mine, g0, s1, s2, s3):
    zl = idx[2]
    lane = lax.broadcasted_iota(jnp.int32, (32, 128), 1)
    for k, out in enumerate((mine, s1, s2, s3)):
        rows = at((zl + k) % 4 * 32, 32, 32)
        total = own[rows, :] + g1[rows, :].astype(F32) + g2[rows, :].astype(F32) + g3[rows, :].astype(F32)
        back = (4 - k) % 4
        gain_term = jnp.sum(total * w[back * 32 : (back + 1) * 32, :].astype(F32), axis=-1, keepdims=True)
        if k == 0:
            mine[...] = total
            g0[...] = jnp.broadcast_to(gain_term, (32, 128))
        else:
            out[:, :2048] = total.astype(BF16)
            high = gain_term.astype(BF16).astype(F32)
            out[:, 2048:] = jnp.where(lane == 0, high, jnp.where(lane == 1, gain_term - high, 0.0)).astype(BF16)


def z_sum_kernel(idx, mine, g0, s1, s2, s3, out, gain_out):
    out[...] = (mine[...] + s1[:, :2048].astype(F32) + s2[:, :2048].astype(F32) + s3[:, :2048].astype(F32)) * (1.0 / 64)
    tail = s1[:, 2048:].astype(F32) + s2[:, 2048:].astype(F32) + s3[:, 2048:].astype(F32)
    gain_out[...] = g0[...] + jnp.sum(tail, axis=-1, keepdims=True)


def program(hidden, gain, w_value, d_value):
    flat = lax.axis_index("dp") * 4 + lax.axis_index("pipe")
    idx = (flat // jnp.array([64, 4, 16, 2, 1])) % jnp.array([4, 4, 4, 2, 2])
    zh, c = idx[3], idx[4]
    d, w = d_value[0], w_value[0]
    gain_row = gain.reshape(1, 2048)

    d0, d1 = d[:128], d[128:]
    l0 = send(d0, dx=1)
    r1 = send(d1, dx=3)
    w1, w2, w3 = (send(w, dl=k) for k in (1, 2, 3))
    l1 = send(d1, dx=1)
    r0 = send(d0, dx=3)

    e_own, e1, e2, e3 = call(
        norm_kernel, [((256, 512), BF16)] + [((128, 512), BF16)] * 3, 3_000_000, idx, hidden, gain_row,
        scratch=[pltpu.VMEM((256, 128), F32)],
    )
    m1 = send(e1, dx=1)
    m3 = send(e3, dx=3)
    m2 = send(e2, dx=2)
    fa = send(l0, dx=1)
    fb = send(r1, dx=3)
    z_rows = jnp.concatenate([w, w1, w2, w3])
    y1, y3, y2 = (send(z_rows, dy=k) for k in (1, 3, 2))
    oth = send(jnp.stack([m1, m2, m3]), dc=1)

    keep, give = call(
        encoded_grad_kernel, [((4, 128, 512), F32)] * 2, 2_147_000_000,
        idx, z_rows, y1, y2, y3, d0, d1, l0, l1, fa, fb, r0, r1, scratch=[pltpu.VMEM((512, 2048), BF16)],
    )
    got = send(give, dc=1)
    v_own, v1, v2, v3 = call(
        value_kernel, [((128, 2048), F32)] + [((128, 2048), BF16)] * 3, 2_147_000_000,
        idx, e_own, m1, m2, m3, oth, d0, d1, l0, l1, fa, fb, r0, r1, scratch=[pltpu.VMEM((512, 256), F32)],
    )
    own, give = call(core_sum_kernel, [((4, 64, 512), F32), ((4, 64, 512), BF16)], 1_000_000, idx, keep, got)
    got = send(give, dh=1)
    v1, v3, v2 = send(v1, dy=1), send(v3, dy=3), send(v2, dy=2)
    t0, t1, t2, t3 = call(half_sum_kernel, [((64, 512), F32)] * 4, 1_000_000, idx, own, got)
    t1, t3, t2 = send(t1, dx=3), send(t3, dx=1), send(t2, dx=2)
    mine, g0, s1, s2, s3 = call(
        y_sum_kernel, [((32, 2048), F32), ((32, 128), F32)] + [((32, 2176), BF16)] * 3, 1_000_000,
        idx, v_own, v1, v2, v3, z_rows,
    )
    s1, s2, s3 = send(s1, dl=1), send(s2, dl=2), send(s3, dl=3)
    (result,) = call(norm_backward_kernel, [((64, 2048), BF16)], 1_000_000, idx, hidden, gain_row, t0, t1, t2, t3)
    across = send(result, dh=1)
    result_c = send(result, dc=1)
    grad_value, g = call(z_sum_kernel, [((32, 2048), F32), ((32, 128), F32)], 1_000_000, idx, mine, g0, s1, s2, s3)
    g = g + send(g, dc=1)
    across_c = send(across, dc=1)
    g = g + send(g, dh=1)

    same = jnp.where(zh == 0, jnp.stack([result, across]), jnp.stack([across, result]))
    other = jnp.where(zh == 0, jnp.stack([result_c, across_c]), jnp.stack([across_c, result_c]))
    grad_hidden = jnp.where(c == 0, jnp.stack([same, other]), jnp.stack([other, same])).reshape(256, 2048)
    grad_gain = g[:, 0] / (64 * lax.dynamic_slice(gain, (flat // 4 * 32,), (32,)))
    return (grad_hidden, grad_gain, grad_value[None])


def solution(mesh):
    return jax.shard_map(
        program,
        mesh=mesh,
        in_specs=(P("dp", None), P(), P("pipe", "dp", None), P("pipe", "dp", None)),
        out_specs=(P("dp", None), P("dp"), P("pipe", "dp", None)),
        check_vma=False,
    )
```

time: 899 us -> 148 us (0.16)
  the two profiles are of different devices: /device:TPU:0 before, /device:TPU:41 now
where the time goes in v1:
time: 148 us
  starting transfers between devices  66.4 us (45%)
  waiting for transfers between devices  52.3 us (35%)
  Pallas kernels  20.4 us (14%)
  local copies, waits for them, and re-layouts  4.37 us (3%)
  other arithmetic  2.32 us (2%)
  between operations  2.08 us (1%)
    ppermute x32, starting transfers between devices, send(): return lax.ppermute(value, AXES, pairs(**shift))  66.4 us
    ppermute x32, waiting for transfers between devices, send(): return lax.ppermute(value, AXES, pairs(**shift))  52.3 us
    pallas_call x8, Pallas kernels, call(): pl.pallas_call(body, out_shape=shapes, in_specs=[SMEM] + [VMEM] * (len(ar...  20.4 us
  transfers between devices with their start and end apart: 32, of which 16 were waited for; matrix products, arithmetic and copies ran while one was open for 2% of the time, Pallas kernels for 9%

profile of v1, /device:TPU:41, one launch (start us, length us, event | category | flops | bytes accessed | tf_op | source)
XLA Modules:
  0.0 147.9 jit_solution(16537555272957385233)
XLA Ops:
  0.6 1.7 %collective-permute-start = (bf16[32,2048]{1,0:T(8,128)(2,1)}, bf16[32,2048]{1,0:T(8,128)(2,1)S(1)}, u32[]{:S(2)}, u32[]{:S(2)}) collective-permute-start(bf16[32,2048]{1,0:T(8,128)(2,1)} %bitcast.27), channel_id=1, source_target_pairs={{0,16},{1,17},{2,18},{3,19},{4,20},{5,21},{6,22},{7,23},{8,24},{9,... | collective-permute-start | bytes 393224 | tf_op jit(solution)/shard_map/ppermute | solution.py:29
  3.6 2.6 %collective-permute-start.9 = (bf16[128,2048]{1,0:T(8,128)(2,1)S(1)}, bf16[128,2048]{1,0:T(8,128)(2,1)S(1)}, u32[]{:S(2)}, u32[]{:S(2)}) collective-permute-start(bf16[128,2048]{1,0:T(8,128)(2,1)S(1)} %get-tuple-element.49.d1), channel_id=1, source_target_pairs={{0,192},{1,193},{2,194},{3,195},{4,196},{5,197},{6,198},{7,199},{8... | collective-permute-start | bytes 1572872 | tf_op jit(solution)/shard_map/ppermute | solution.py:29
  6.2 2.7 %collective-permute-start.11 = (bf16[128,2048]{1,0:T(8,128)(2,1)S(1)}, bf16[128,2048]{1,0:T(8,128)(2,1)S(1)}, u32[]{:S(2)}, u32[]{:S(2)}) collective-permute-start(bf16[128,2048]{1,0:T(8,128)(2,1)S(1)} %get-tuple-element.50.d0), channel_id=1, source_target_pairs={{0,192},{1,193},{2,194},{3,195},{4,196},{5,197},{6,198},{7,199},{8... | collective-permute-start | bytes 1572872 | tf_op jit(solution)/shard_map/ppermute | solution.py:29
  8.9 1.5 collective-permute-start.1
  10.3 3.7 %collective-permute-done.1 = bf16[32,2048]{1,0:T(8,128)(2,1)S(1)} collective-permute-done((bf16[32,2048]{1,0:T(8,128)(2,1)S(1)}, bf16[32,2048]{1,0:T(8,128)(2,1)S(1)}, u32[]{:S(2)}, u32[]{:S(2)}) %collective-permute-start.1) | collective-permute-done | bytes 131104 | tf_op jit(solution)/shard_map/ppermute | solution.py:29
  14.0 3.8 %collective-permute-start.2 = (bf16[32,2048]{1,0:T(8,128)(2,1)S(1)}, bf16[32,2048]{1,0:T(8,128)(2,1)S(1)}, u32[]{:S(2)}, u32[]{:S(2)}) collective-permute-start(bf16[32,2048]{1,0:T(8,128)(2,1)S(1)} %bitcast.29), channel_id=1, source_target_pairs={{0,48},{1,49},{2,50},{3,51},{4,52},{5,53},{6,54},{7,55},{8,56},{9,... | collective-permute-start | bytes 393224 | tf_op jit(solution)/shard_map/ppermute | solution.py:29
  17.8 1.9 %collective-permute-done.2 = bf16[32,2048]{1,0:T(8,128)(2,1)S(1)} collective-permute-done((bf16[32,2048]{1,0:T(8,128)(2,1)S(1)}, bf16[32,2048]{1,0:T(8,128)(2,1)S(1)}, u32[]{:S(2)}, u32[]{:S(2)}) %collective-permute-start.2) | collective-permute-done | bytes 131104 | tf_op jit(solution)/shard_map/ppermute | solution.py:29
  19.8 1.4 collective-permute-start.3
  22.0 2.0 %collective-permute-start.5 = (bf16[128,2048]{1,0:T(8,128)(2,1)S(1)}, bf16[128,2048]{1,0:T(8,128)(2,1)}, u32[]{:S(2)}, u32[]{:S(2)}) collective-permute-start(bf16[128,2048]{1,0:T(8,128)(2,1)S(1)} %pad_maximum_fusion.w0.w), channel_id=1, source_target_pairs={{0,12},{1,13},{2,14},{3,15},{4,0},{5,1},{6,2},{7,3},{8,4},{9,5},{1... | collective-permute-start | bytes 1572872 | tf_op jit(solution)/shard_map/ppermute | solution.py:29
  24.0 3.8 %collective-permute-done.11.r0 = bf16[128,2048]{1,0:T(8,128)(2,1)S(1)} collective-permute-done((bf16[128,2048]{1,0:T(8,128)(2,1)S(1)}, bf16[128,2048]{1,0:T(8,128)(2,1)S(1)}, u32[]{:S(2)}, u32[]{:S(2)}) %collective-permute-start.11) | collective-permute-done | bytes 524320 | tf_op jit(solution)/shard_map/ppermute | solution.py:29
  27.7 3.4 %collective-permute-start.10 = (bf16[128,2048]{1,0:T(8,128)(2,1)S(1)}, bf16[128,2048]{1,0:T(8,128)(2,1)}, u32[]{:S(2)}, u32[]{:S(2)}) collective-permute-start(bf16[128,2048]{1,0:T(8,128)(2,1)S(1)} %collective-permute-done.9.r1), channel_id=1, source_target_pairs={{0,192},{1,193},{2,194},{3,195},{4,196},{5,197},{6,198},{7,199},{8... | collective-permute-start | bytes 1572872 | tf_op jit(solution)/shard_map/ppermute | solution.py:29
  33.5 13.1 %collective-permute-done.5.w3 = bf16[128,2048]{1,0:T(8,128)(2,1)} collective-permute-done((bf16[128,2048]{1,0:T(8,128)(2,1)S(1)}, bf16[128,2048]{1,0:T(8,128)(2,1)}, u32[]{:S(2)}, u32[]{:S(2)}) %collective-permute-start.5) | collective-permute-done | bytes 524320 | tf_op jit(solution)/shard_map/ppermute | solution.py:29
  47.6 7.5 %shard_map.85 = (f32[4,128,512]{2,1,0:T(8,128)S(1)}, f32[4,128,512]{2,1,0:T(8,128)S(1)}) custom-call(s32[5]{0:T(128)S(1)} %and_select_fusion.idx, bf16[128,2048]{1,0:T(8,128)(2,1)S(1)} %pad_maximum_fusion.w0.w, bf16[128,2048]{1,0:T(8,128)(2,1)} %collective-permute-done.3.w1, bf16[128,2048]{1,0:T(8,128)(2,1)} %collective-permute-done.4.w2, ...), custom_call_target="tpu_custom_call" | custom-call | flops 2147000064 | bytes 8388628 | tf_op jit(solution)/shard_map/pallas_call | solution.py:35
  57.7 2.8 %collective-permute-start.21 = (bf16[128,512]{1,0:T(8,128)(2,1)S(1)}, bf16[128,512]{1,0:T(8,128)(2,1)S(1)}, u32[]{:S(2)}, u32[]{:S(2)}) collective-permute-start(bf16[128,512]{1,0:T(8,128)(2,1)S(1)} %get-tuple-element.36), channel_id=1, source_target_pairs={{0,128},{1,129},{2,130},{3,131},{4,132},{5,133},{6,134},{7,135},{8... | collective-permute-start | bytes 393224 | tf_op jit(solution)/shard_map/ppermute | solution.py:29
  60.5 1.6 %collective-permute-start.22 = (bf16[128,512]{1,0:T(8,128)(2,1)S(1)}, bf16[128,512]{1,0:T(8,128)(2,1)S(1)}, u32[]{:S(2)}, u32[]{:S(2)}) collective-permute-start(bf16[128,512]{1,0:T(8,128)(2,1)S(1)} %get-tuple-element.37), channel_id=1, source_target_pairs={{0,192},{1,193},{2,194},{3,195},{4,196},{5,197},{6,198},{7,199},{8... | collective-permute-start | bytes 393224 | tf_op jit(solution)/shard_map/ppermute | solution.py:29
  62.1 1.8 %collective-permute-done.20.m1 = bf16[128,512]{1,0:T(8,128)(2,1)S(1)} collective-permute-done((bf16[128,512]{1,0:T(8,128)(2,1)S(1)}, bf16[128,512]{1,0:T(8,128)(2,1)S(1)}, u32[]{:S(2)}, u32[]{:S(2)}) %collective-permute-start.20) | collective-permute-done | bytes 131104 | tf_op jit(solution)/shard_map/ppermute | solution.py:29
  63.9 3.0 %collective-permute-done.21.m2 = bf16[128,512]{1,0:T(8,128)(2,1)S(1)} collective-permute-done((bf16[128,512]{1,0:T(8,128)(2,1)S(1)}, bf16[128,512]{1,0:T(8,128)(2,1)S(1)}, u32[]{:S(2)}, u32[]{:S(2)}) %collective-permute-start.21) | collective-permute-done | bytes 131104 | tf_op jit(solution)/shard_map/ppermute | solution.py:29
  68.3 1.3 collective-permute-done.23.oth
  69.6 7.5 %shard_map.90 = (f32[128,2048]{1,0:T(8,128)S(1)}, bf16[128,2048]{1,0:T(8,128)(2,1)S(1)}, bf16[128,2048]{1,0:T(8,128)(2,1)S(1)}, bf16[128,2048]{1,0:T(8,128)(2,1)S(1)}) custom-call(s32[5]{0:T(128)S(1)} %and_select_fusion.idx, bf16[256,512]{1,0:T(8,128)(2,1)S(1)} %get-tuple-element.34.e_own, bf16[128,512]{1,0:T(8,128)(2,1)S(1)} %collective-permute-done.20.m1, ...), custom_call_target="tpu_custom_call" | custom-call | flops 2147000064 | bytes 7864340 | tf_op jit(solution)/shard_map/pallas_call | solution.py:35
  79.5 1.8 %collective-permute-start.26 = (bf16[128,2048]{1,0:T(8,128)(2,1)S(1)}, bf16[128,2048]{1,0:T(8,128)(2,1)S(1)}, u32[]{:S(2)}, u32[]{:S(2)}) collective-permute-start(bf16[128,2048]{1,0:T(8,128)(2,1)S(1)} %get-tuple-element.41), channel_id=1, source_target_pairs={{0,12},{1,13},{2,14},{3,15},{4,0},{5,1},{6,2},{7,3},{8,4},{9,5},{1... | collective-permute-start | bytes 1572872 | tf_op jit(solution)/shard_map/ppermute | solution.py:29
  82.0 5.2 %collective-permute-start.13 = (bf16[4,64,512]{2,1,0:T(8,128)(2,1)S(1)}, bf16[4,64,512]{2,1,0:T(8,128)(2,1)S(1)}, u32[]{:S(2)}, u32[]{:S(2)}) collective-permute-start(bf16[4,64,512]{2,1,0:T(8,128)(2,1)S(1)} %get-tuple-element.29), channel_id=1, source_target_pairs={{0,2},{1,3},{2,0},{3,1},{4,6},{5,7},{6,4},{7,5},{8,10},{9,11},{10,... | collective-permute-start | bytes 786440 | tf_op jit(solution)/shard_map/ppermute | solution.py:29
  87.2 5.4 %collective-permute-done.13.got = bf16[4,64,512]{2,1,0:T(8,128)(2,1)S(1)} collective-permute-done((bf16[4,64,512]{2,1,0:T(8,128)(2,1)S(1)}, bf16[4,64,512]{2,1,0:T(8,128)(2,1)S(1)}, u32[]{:S(2)}, u32[]{:S(2)}) %collective-permute-start.13) | collective-permute-done | bytes 262176 | tf_op jit(solution)/shard_map/ppermute | solution.py:29
  93.2 3.7 %collective-permute-start.14 = (f32[64,512]{1,0:T(8,128)S(1)}, f32[64,512]{1,0:T(8,128)S(1)}, u32[]{:S(2)}, u32[]{:S(2)}) collective-permute-start(f32[64,512]{1,0:T(8,128)S(1)} %get-tuple-element.31), channel_id=1, source_target_pairs={{0,192},{1,193},{2,194},{3,195},{4,196},{5,197},{6,198},{7,199},{8... | collective-permute-start | bytes 393224 | tf_op jit(solution)/shard_map/ppermute | solution.py:29
  97.8 6.4 %collective-permute-done.26.g3 = bf16[128,2048]{1,0:T(8,128)(2,1)S(1)} collective-permute-done((bf16[128,2048]{1,0:T(8,128)(2,1)S(1)}, bf16[128,2048]{1,0:T(8,128)(2,1)S(1)}, u32[]{:S(2)}, u32[]{:S(2)}) %collective-permute-start.26) | collective-permute-done | bytes 524320 | tf_op jit(solution)/shard_map/ppermute | solution.py:29
  105.1 1.4 collective-permute-start.27
  106.5 3.1 %collective-permute-start.28 = (bf16[32,2176]{1,0:T(8,128)(2,1)S(1)}, bf16[32,2176]{1,0:T(8,128)(2,1)S(1)}, u32[]{:S(2)}, u32[]{:S(2)}) collective-permute-start(bf16[32,2176]{1,0:T(8,128)(2,1)S(1)} %get-tuple-element.45), channel_id=1, source_target_pairs={{0,32},{1,33},{2,34},{3,35},{4,36},{5,37},{6,38},{7,39},{8,40},{9,... | collective-permute-start | bytes 417800 | tf_op jit(solution)/shard_map/ppermute | solution.py:29
  110.9 6.9 %collective-permute-start.17 = (bf16[64,2048]{1,0:T(8,128)(2,1)S(1)}, bf16[64,2048]{1,0:T(8,128)(2,1)S(1)}, u32[]{:S(2)}, u32[]{:S(2)}) collective-permute-start(bf16[64,2048]{1,0:T(8,128)(2,1)S(1)} %shard_map.88), channel_id=1, source_target_pairs={{0,2},{1,3},{2,0},{3,1},{4,6},{5,7},{6,4},{7,5},{8,10},{9,11},{10,... | collective-permute-start | bytes 786440 | tf_op jit(solution)/shard_map/ppermute | solution.py:29
  117.9 8.2 %collective-permute-done.28.s2 = bf16[32,2176]{1,0:T(8,128)(2,1)S(1)} collective-permute-done((bf16[32,2176]{1,0:T(8,128)(2,1)S(1)}, bf16[32,2176]{1,0:T(8,128)(2,1)S(1)}, u32[]{:S(2)}, u32[]{:S(2)}) %collective-permute-start.28) | collective-permute-done | bytes 139296 | tf_op jit(solution)/shard_map/ppermute | solution.py:29
  126.1 1.4 collective-permute-done.29.s3
  127.5 1.3 shard_map.92
  128.8 1.4 collective-permute-start.30
  131.1 11.4 %collective-permute-start.31 = (f32[32,128]{1,0:T(8,128)S(1)}, f32[32,128]{1,0:T(8,128)S(1)}, u32[]{:S(2)}, u32[]{:S(2)}) collective-permute-start(f32[32,128]{1,0:T(8,128)S(1)} %add.20), channel_id=1, source_target_pairs={{0,2},{1,3},{2,0},{3,1},{4,6},{5,7},{6,4},{7,5},{8,10},{9,11},{10,... | collective-permute-start | bytes 49160 | tf_op jit(solution)/shard_map/ppermute | solution.py:29
  (65 shorter events, 21.1 us)
Async XLA Ops:
  0.6 8.2 %collective-permute-start = (bf16[32,2048]{1,0:T(8,128)(2,1)}, bf16[32,2048]{1,0:T(8,128)(2,1)S(1)}, u32[]{:S(2)}, u32[]{:S(2)}) collective-permute-start(bf16[32,2048]{1,0:T(8,128)(2,1)} %bitcast.27), channel_id=1, source_target_pairs={{0,16},{1,17},{2,18},{3,19},{4,20},{5,21},{6,22},{7,23},{8,24},{9,... | collective-permute-start | bytes 393224 | tf_op jit(solution)/shard_map/ppermute | solution.py:29
  3.6 17.6 %collective-permute-start.9 = (bf16[128,2048]{1,0:T(8,128)(2,1)S(1)}, bf16[128,2048]{1,0:T(8,128)(2,1)S(1)}, u32[]{:S(2)}, u32[]{:S(2)}) collective-permute-start(bf16[128,2048]{1,0:T(8,128)(2,1)S(1)} %get-tuple-element.49.d1), channel_id=1, source_target_pairs={{0,192},{1,193},{2,194},{3,195},{4,196},{5,197},{6,198},{7,199},{8... | collective-permute-start | bytes 1572872 | tf_op jit(solution)/shard_map/ppermute | solution.py:29
  6.2 15.8 %collective-permute-start.6 = (bf16[128,2048]{1,0:T(8,128)(2,1)S(1)}, bf16[128,2048]{1,0:T(8,128)(2,1)S(1)}, u32[]{:S(2)}, u32[]{:S(2)}) collective-permute-start(bf16[128,2048]{1,0:T(8,128)(2,1)S(1)} %get-tuple-element.50.d0), channel_id=1, source_target_pairs={{0,64},{1,65},{2,66},{3,67},{4,68},{5,69},{6,70},{7,71},{8,72},{9,... | collective-permute-start | bytes 1572872 | tf_op jit(solution)/shard_map/ppermute | solution.py:29
  6.2 21.6 %collective-permute-start.11 = (bf16[128,2048]{1,0:T(8,128)(2,1)S(1)}, bf16[128,2048]{1,0:T(8,128)(2,1)S(1)}, u32[]{:S(2)}, u32[]{:S(2)}) collective-permute-start(bf16[128,2048]{1,0:T(8,128)(2,1)S(1)} %get-tuple-element.50.d0), channel_id=1, source_target_pairs={{0,192},{1,193},{2,194},{3,195},{4,196},{5,197},{6,198},{7,199},{8... | collective-permute-start | bytes 1572872 | tf_op jit(solution)/shard_map/ppermute | solution.py:29
  8.9 22.3 %collective-permute-start.7 = (bf16[128,2048]{1,0:T(8,128)(2,1)S(1)}, bf16[128,2048]{1,0:T(8,128)(2,1)S(1)}, u32[]{:S(2)}, u32[]{:S(2)}) collective-permute-start(bf16[128,2048]{1,0:T(8,128)(2,1)S(1)} %get-tuple-element.49.d1), channel_id=1, source_target_pairs={{0,64},{1,65},{2,66},{3,67},{4,68},{5,69},{6,70},{7,71},{8,72},{9,... | collective-permute-start | bytes 1572872 | tf_op jit(solution)/shard_map/ppermute | solution.py:29
  8.9 5.1 %collective-permute-start.1 = (bf16[32,2048]{1,0:T(8,128)(2,1)S(1)}, bf16[32,2048]{1,0:T(8,128)(2,1)S(1)}, u32[]{:S(2)}, u32[]{:S(2)}) collective-permute-start(bf16[32,2048]{1,0:T(8,128)(2,1)S(1)} %bitcast.28), channel_id=1, source_target_pairs={{0,32},{1,33},{2,34},{3,35},{4,36},{5,37},{6,38},{7,39},{8,40},{9,... | collective-permute-start | bytes 393224 | tf_op jit(solution)/shard_map/ppermute | solution.py:29
  14.0 5.8 %collective-permute-start.2 = (bf16[32,2048]{1,0:T(8,128)(2,1)S(1)}, bf16[32,2048]{1,0:T(8,128)(2,1)S(1)}, u32[]{:S(2)}, u32[]{:S(2)}) collective-permute-start(bf16[32,2048]{1,0:T(8,128)(2,1)S(1)} %bitcast.29), channel_id=1, source_target_pairs={{0,48},{1,49},{2,50},{3,51},{4,52},{5,53},{6,54},{7,55},{8,56},{9,... | collective-permute-start | bytes 393224 | tf_op jit(solution)/shard_map/ppermute | solution.py:29
  19.8 13.1 %collective-permute-start.3 = (bf16[128,2048]{1,0:T(8,128)(2,1)S(1)}, bf16[128,2048]{1,0:T(8,128)(2,1)}, u32[]{:S(2)}, u32[]{:S(2)}) collective-permute-start(bf16[128,2048]{1,0:T(8,128)(2,1)S(1)} %pad_maximum_fusion.w0.w), channel_id=1, source_target_pairs={{0,4},{1,5},{2,6},{3,7},{4,8},{5,9},{6,10},{7,11},{8,12},{9,13},{1... | collective-permute-start | bytes 1572872 | tf_op jit(solution)/shard_map/ppermute | solution.py:29
  21.2 12.3 %collective-permute-start.4 = (bf16[128,2048]{1,0:T(8,128)(2,1)S(1)}, bf16[128,2048]{1,0:T(8,128)(2,1)}, u32[]{:S(2)}, u32[]{:S(2)}) collective-permute-start(bf16[128,2048]{1,0:T(8,128)(2,1)S(1)} %pad_maximum_fusion.w0.w), channel_id=1, source_target_pairs={{0,8},{1,9},{2,10},{3,11},{4,12},{5,13},{6,14},{7,15},{8,0},{9,1},... | collective-permute-start | bytes 1572872 | tf_op jit(solution)/shard_map/ppermute | solution.py:29
  22.0 24.5 %collective-permute-start.5 = (bf16[128,2048]{1,0:T(8,128)(2,1)S(1)}, bf16[128,2048]{1,0:T(8,128)(2,1)}, u32[]{:S(2)}, u32[]{:S(2)}) collective-permute-start(bf16[128,2048]{1,0:T(8,128)(2,1)S(1)} %pad_maximum_fusion.w0.w), channel_id=1, source_target_pairs={{0,12},{1,13},{2,14},{3,15},{4,0},{5,1},{6,2},{7,3},{8,4},{9,5},{1... | collective-permute-start | bytes 1572872 | tf_op jit(solution)/shard_map/ppermute | solution.py:29
  27.7 18.8 %collective-permute-start.10 = (bf16[128,2048]{1,0:T(8,128)(2,1)S(1)}, bf16[128,2048]{1,0:T(8,128)(2,1)}, u32[]{:S(2)}, u32[]{:S(2)}) collective-permute-start(bf16[128,2048]{1,0:T(8,128)(2,1)S(1)} %collective-permute-done.9.r1), channel_id=1, source_target_pairs={{0,192},{1,193},{2,194},{3,195},{4,196},{5,197},{6,198},{7,199},{8... | collective-permute-start | bytes 1572872 | tf_op jit(solution)/shard_map/ppermute | solution.py:29
  32.0 14.6 %collective-permute-start.8 = (bf16[128,2048]{1,0:T(8,128)(2,1)S(1)}, bf16[128,2048]{1,0:T(8,128)(2,1)}, u32[]{:S(2)}, u32[]{:S(2)}) collective-permute-start(bf16[128,2048]{1,0:T(8,128)(2,1)S(1)} %collective-permute-done.6.l0), channel_id=1, source_target_pairs={{0,64},{1,65},{2,66},{3,67},{4,68},{5,69},{6,70},{7,71},{8,72},{9,... | collective-permute-start | bytes 1572872 | tf_op jit(solution)/shard_map/ppermute | solution.py:29
  55.1 26.2 %collective-permute-start.12 = (f32[4,128,512]{2,1,0:T(8,128)S(1)}, f32[4,128,512]{2,1,0:T(8,128)S(1)}, u32[]{:S(2)}, u32[]{:S(2)}) collective-permute-start(f32[4,128,512]{2,1,0:T(8,128)S(1)} %get-tuple-element.27), channel_id=1, source_target_pairs={{0,1},{1,0},{2,3},{3,2},{4,5},{5,4},{6,7},{7,6},{8,9},{9,8},{10,11... | collective-permute-start | bytes 3145736 | tf_op jit(solution)/shard_map/ppermute | solution.py:29
  57.4 6.5 %collective-permute-start.20 = (bf16[128,512]{1,0:T(8,128)(2,1)S(1)}, bf16[128,512]{1,0:T(8,128)(2,1)S(1)}, u32[]{:S(2)}, u32[]{:S(2)}) collective-permute-start(bf16[128,512]{1,0:T(8,128)(2,1)S(1)} %get-tuple-element.35), channel_id=1, source_target_pairs={{0,64},{1,65},{2,66},{3,67},{4,68},{5,69},{6,70},{7,71},{8,72},{9,... | collective-permute-start | bytes 393224 | tf_op jit(solution)/shard_map/ppermute | solution.py:29
  57.7 9.2 %collective-permute-start.21 = (bf16[128,512]{1,0:T(8,128)(2,1)S(1)}, bf16[128,512]{1,0:T(8,128)(2,1)S(1)}, u32[]{:S(2)}, u32[]{:S(2)}) collective-permute-start(bf16[128,512]{1,0:T(8,128)(2,1)S(1)} %get-tuple-element.36), channel_id=1, source_target_pairs={{0,128},{1,129},{2,130},{3,131},{4,132},{5,133},{6,134},{7,135},{8... | collective-permute-start | bytes 393224 | tf_op jit(solution)/shard_map/ppermute | solution.py:29
  60.5 6.5 %collective-permute-start.22 = (bf16[128,512]{1,0:T(8,128)(2,1)S(1)}, bf16[128,512]{1,0:T(8,128)(2,1)S(1)}, u32[]{:S(2)}, u32[]{:S(2)}) collective-permute-start(bf16[128,512]{1,0:T(8,128)(2,1)S(1)} %get-tuple-element.37), channel_id=1, source_target_pairs={{0,192},{1,193},{2,194},{3,195},{4,196},{5,197},{6,198},{7,199},{8... | collective-permute-start | bytes 393224 | tf_op jit(solution)/shard_map/ppermute | solution.py:29
  67.0 2.6 %collective-permute-start.23 = (bf16[3,128,512]{2,1,0:T(8,128)(2,1)S(1)}, bf16[3,128,512]{2,1,0:T(8,128)(2,1)S(1)}, u32[]{:S(2)}, u32[]{:S(2)}) collective-permute-start(bf16[3,128,512]{2,1,0:T(8,128)(2,1)S(1)} %pad_maximum_fusion.1), channel_id=1, source_target_pairs={{0,1},{1,0},{2,3},{3,2},{4,5},{5,4},{6,7},{7,6},{8,9},{9,8},{10,11... | collective-permute-start | bytes 1179656 | tf_op jit(solution)/shard_map/ppermute | solution.py:29
  77.1 20.6 %collective-permute-start.24 = (bf16[128,2048]{1,0:T(8,128)(2,1)S(1)}, bf16[128,2048]{1,0:T(8,128)(2,1)S(1)}, u32[]{:S(2)}, u32[]{:S(2)}) collective-permute-start(bf16[128,2048]{1,0:T(8,128)(2,1)S(1)} %get-tuple-element.39), channel_id=1, source_target_pairs={{0,4},{1,5},{2,6},{3,7},{4,8},{5,9},{6,10},{7,11},{8,12},{9,13},{1... | collective-permute-start | bytes 1572872 | tf_op jit(solution)/shard_map/ppermute | solution.py:29
  78.4 19.4 %collective-permute-start.25 = (bf16[128,2048]{1,0:T(8,128)(2,1)S(1)}, bf16[128,2048]{1,0:T(8,128)(2,1)S(1)}, u32[]{:S(2)}, u32[]{:S(2)}) collective-permute-start(bf16[128,2048]{1,0:T(8,128)(2,1)S(1)} %get-tuple-element.40), channel_id=1, source_target_pairs={{0,8},{1,9},{2,10},{3,11},{4,12},{5,13},{6,14},{7,15},{8,0},{9,1},... | collective-permute-start | bytes 1572872 | tf_op jit(solution)/shard_map/ppermute | solution.py:29
  79.5 24.7 %collective-permute-start.26 = (bf16[128,2048]{1,0:T(8,128)(2,1)S(1)}, bf16[128,2048]{1,0:T(8,128)(2,1)S(1)}, u32[]{:S(2)}, u32[]{:S(2)}) collective-permute-start(bf16[128,2048]{1,0:T(8,128)(2,1)S(1)} %get-tuple-element.41), channel_id=1, source_target_pairs={{0,12},{1,13},{2,14},{3,15},{4,0},{5,1},{6,2},{7,3},{8,4},{9,5},{1... | collective-permute-start | bytes 1572872 | tf_op jit(solution)/shard_map/ppermute | solution.py:29
  82.0 10.7 %collective-permute-start.13 = (bf16[4,64,512]{2,1,0:T(8,128)(2,1)S(1)}, bf16[4,64,512]{2,1,0:T(8,128)(2,1)S(1)}, u32[]{:S(2)}, u32[]{:S(2)}) collective-permute-start(bf16[4,64,512]{2,1,0:T(8,128)(2,1)S(1)} %get-tuple-element.29), channel_id=1, source_target_pairs={{0,2},{1,3},{2,0},{3,1},{4,6},{5,7},{6,4},{7,5},{8,10},{9,11},{10,... | collective-permute-start | bytes 786440 | tf_op jit(solution)/shard_map/ppermute | solution.py:29
  93.2 16.4 %collective-permute-start.14 = (f32[64,512]{1,0:T(8,128)S(1)}, f32[64,512]{1,0:T(8,128)S(1)}, u32[]{:S(2)}, u32[]{:S(2)}) collective-permute-start(f32[64,512]{1,0:T(8,128)S(1)} %get-tuple-element.31), channel_id=1, source_target_pairs={{0,192},{1,193},{2,194},{3,195},{4,196},{5,197},{6,198},{7,199},{8... | collective-permute-start | bytes 393224 | tf_op jit(solution)/shard_map/ppermute | solution.py:29
  97.0 13.1 %collective-permute-start.15 = (f32[64,512]{1,0:T(8,128)S(1)}, f32[64,512]{1,0:T(8,128)S(1)}, u32[]{:S(2)}, u32[]{:S(2)}) collective-permute-start(f32[64,512]{1,0:T(8,128)S(1)} %get-tuple-element.32), channel_id=1, source_target_pairs={{0,128},{1,129},{2,130},{3,131},{4,132},{5,133},{6,134},{7,135},{8... | collective-permute-start | bytes 393224 | tf_op jit(solution)/shard_map/ppermute | solution.py:29
  97.8 12.3 %collective-permute-start.16 = (f32[64,512]{1,0:T(8,128)S(1)}, f32[64,512]{1,0:T(8,128)S(1)}, u32[]{:S(2)}, u32[]{:S(2)}) collective-permute-start(f32[64,512]{1,0:T(8,128)S(1)} %get-tuple-element.33), channel_id=1, source_target_pairs={{0,64},{1,65},{2,66},{3,67},{4,68},{5,69},{6,70},{7,71},{8,72},{9,... | collective-permute-start | bytes 393224 | tf_op jit(solution)/shard_map/ppermute | solution.py:29
  105.1 12.8 %collective-permute-start.27 = (bf16[32,2176]{1,0:T(8,128)(2,1)S(1)}, bf16[32,2176]{1,0:T(8,128)(2,1)S(1)}, u32[]{:S(2)}, u32[]{:S(2)}) collective-permute-start(bf16[32,2176]{1,0:T(8,128)(2,1)S(1)} %get-tuple-element.44), channel_id=1, source_target_pairs={{0,16},{1,17},{2,18},{3,19},{4,20},{5,21},{6,22},{7,23},{8,24},{9,... | collective-permute-start | bytes 417800 | tf_op jit(solution)/shard_map/ppermute | solution.py:29
  106.5 19.6 %collective-permute-start.28 = (bf16[32,2176]{1,0:T(8,128)(2,1)S(1)}, bf16[32,2176]{1,0:T(8,128)(2,1)S(1)}, u32[]{:S(2)}, u32[]{:S(2)}) collective-permute-start(bf16[32,2176]{1,0:T(8,128)(2,1)S(1)} %get-tuple-element.45), channel_id=1, source_target_pairs={{0,32},{1,33},{2,34},{3,35},{4,36},{5,37},{6,38},{7,39},{8,40},{9,... | collective-permute-start | bytes 417800 | tf_op jit(solution)/shard_map/ppermute | solution.py:29
  109.6 17.9 %collective-permute-start.29 = (bf16[32,2176]{1,0:T(8,128)(2,1)S(1)}, bf16[32,2176]{1,0:T(8,128)(2,1)S(1)}, u32[]{:S(2)}, u32[]{:S(2)}) collective-permute-start(bf16[32,2176]{1,0:T(8,128)(2,1)S(1)} %get-tuple-element.46), channel_id=1, source_target_pairs={{0,48},{1,49},{2,50},{3,51},{4,52},{5,53},{6,54},{7,55},{8,56},{9,... | collective-permute-start | bytes 417800 | tf_op jit(solution)/shard_map/ppermute | solution.py:29
  110.9 34.2 %collective-permute-start.17 = (bf16[64,2048]{1,0:T(8,128)(2,1)S(1)}, bf16[64,2048]{1,0:T(8,128)(2,1)S(1)}, u32[]{:S(2)}, u32[]{:S(2)}) collective-permute-start(bf16[64,2048]{1,0:T(8,128)(2,1)S(1)} %shard_map.88), channel_id=1, source_target_pairs={{0,2},{1,3},{2,0},{3,1},{4,6},{5,7},{6,4},{7,5},{8,10},{9,11},{10,... | collective-permute-start | bytes 786440 | tf_op jit(solution)/shard_map/ppermute | solution.py:29
  128.8 2.3 %collective-permute-start.30 = (f32[32,128]{1,0:T(8,128)S(1)}, f32[32,128]{1,0:T(8,128)S(1)}, u32[]{:S(2)}, u32[]{:S(2)}) collective-permute-start(f32[32,128]{1,0:T(8,128)S(1)} %get-tuple-element.47), channel_id=1, source_target_pairs={{0,1},{1,0},{2,3},{3,2},{4,5},{5,4},{6,7},{7,6},{8,9},{9,8},{10,11... | collective-permute-start | bytes 49160 | tf_op jit(solution)/shard_map/ppermute | solution.py:29
  131.1 13.3 %collective-permute-start.31 = (f32[32,128]{1,0:T(8,128)S(1)}, f32[32,128]{1,0:T(8,128)S(1)}, u32[]{:S(2)}, u32[]{:S(2)}) collective-permute-start(f32[32,128]{1,0:T(8,128)S(1)} %add.20), channel_id=1, source_target_pairs={{0,2},{1,3},{2,0},{3,1},{4,6},{5,7},{6,4},{7,5},{8,10},{9,11},{10,... | collective-permute-start | bytes 49160 | tf_op jit(solution)/shard_map/ppermute | solution.py:29
  144.4 1.9 %collective-permute-start.18 = (bf16[64,2048]{1,0:T(8,128)(2,1)S(1)}, bf16[64,2048]{1,0:T(8,128)(2,1)S(1)}, u32[]{:S(2)}, u32[]{:S(2)}) collective-permute-start(bf16[64,2048]{1,0:T(8,128)(2,1)S(1)} %shard_map.88), channel_id=1, source_target_pairs={{0,1},{1,0},{2,3},{3,2},{4,5},{5,4},{6,7},{7,6},{8,9},{9,8},{10,11... | collective-permute-start | bytes 786440 | tf_op jit(solution)/shard_map/ppermute | solution.py:29
  145.1 1.5 %collective-permute-start.19 = (bf16[64,2048]{1,0:T(8,128)(2,1)S(1)}, bf16[64,2048]{1,0:T(8,128)(2,1)S(1)}, u32[]{:S(2)}, u32[]{:S(2)}) collective-permute-start(bf16[64,2048]{1,0:T(8,128)(2,1)S(1)} %collective-permute-done.17), channel_id=1, source_target_pairs={{0,1},{1,0},{2,3},{3,2},{4,5},{5,4},{6,7},{7,6},{8,9},{9,8},{10,11... | collective-permute-start | bytes 786440 | tf_op jit(solution)/shard_map/ppermute | solution.py:29
  (7 other events, 43.7 us)

commit v2 on v1

v2 whole, which is shorter than its diff:
```python
import functools

import jax
import jax.numpy as jnp
from jax import lax
from jax.experimental import pallas as pl
from jax.experimental.pallas import tpu as pltpu
from jax.sharding import PartitionSpec as P


epsilon = 1e-06
F32, BF16 = jnp.float32, jnp.bfloat16
AXES = ("dp", "pipe")
VMEM = pl.BlockSpec(memory_space=pltpu.VMEM)
SMEM = pl.BlockSpec(memory_space=pltpu.SMEM)


def pairs(dx=0, dy=0, dl=0, dh=0, dc=0):
    out = []
    for x in range(4):
        for zl in range(4):
            for y in range(4):
                for zh in range(2):
                    for c in range(2):
                        source = (((x * 4 + zl) * 4 + y) * 2 + zh) * 2 + c
                        target = ((((x + dx) % 4 * 4 + (zl + dl) % 4) * 4 + (y + dy) % 4) * 2 + (zh + dh) % 2) * 2 + (c + dc) % 2
                        out.append((source, target))
    return out


def send(value, **shift):
    return lax.ppermute(value, AXES, pairs(**shift))


def call(body, outs, flops, *args, scratch=(), mib=8):
    shapes = [jax.ShapeDtypeStruct(s, t) for s, t in outs]
    moved = sum(v.size * v.dtype.itemsize for v in args) + sum(v.size * v.dtype.itemsize for v in shapes)
    return pl.pallas_call(
        body,
        out_shape=shapes,
        in_specs=[SMEM] + [VMEM] * (len(args) - 1),
        out_specs=[VMEM] * len(shapes),
        scratch_shapes=list(scratch),
        cost_estimate=pl.CostEstimate(flops=flops, bytes_accessed=moved, transcendentals=0),
        compiler_params=pltpu.CompilerParams(vmem_limit_bytes=mib * 1024 * 1024),
    )(*args)


def at(start, size, multiple):
    return pl.ds(pl.multiple_of(start, multiple), size)


def norm_kernel(idx, h, gain, own, p1, p2, p3, scale):
    x, c = idx[0], idx[4]
    h_all = h[...].astype(F32)
    scale[...] = jnp.broadcast_to(jnp.sqrt(jnp.mean(h_all * h_all, axis=-1, keepdims=True) + epsilon), (256, 128))
    columns = at(x * 512, 512, 512)
    own[...] = (h[:, columns].astype(F32) / scale[:, :1] * gain[:, columns]).T.astype(BF16)
    rows = at(c * 128, 128, 128)
    for k, out in ((1, p1), (2, p2), (3, p3)):
        columns = at((x + k) % 4 * 512, 512, 512)
        out[...] = (h[rows, columns].astype(F32) / scale[rows, :1] * gain[:, columns]).T.astype(BF16)


def dot(a, b, contract=0):
    return lax.dot_general(a, b, (((1,), (contract,)), ((), ())), preferred_element_type=F32)


def value_near_kernel(idx, e_own, m1, m3, oth, d, l, r, acc, e):
    c = idx[4]
    for k, mine, other in ((0, m1, 0), (1, m3, 2)):
        e[:, at(k * 256 + c * 128, 128, 128)] = mine[...]
        e[:, at(k * 256 + (1 - c) * 128, 128, 128)] = oth[other]

    def column(j, carry):
        columns = at(j * 256, 256, 256)
        acc[:, columns] = dot(e_own[...], d[:, columns]) + dot(e[:, :256], l[:, columns]) + dot(e[:, 256:], r[:, columns])
        return carry

    lax.fori_loop(0, 8, column, 0)


def value_far_kernel(start, idx, m2, oth, acc, fa, fb, own, s1, s2, s3, e, tmp):
    y, c = idx[1], idx[4]
    e[:, at(c * 128, 128, 128)] = m2[...]
    e[:, at((1 - c) * 128, 128, 128)] = oth[1]

    def column(j, carry):
        columns, source = at(j * 256, 256, 256), at(start + j * 256, 256, 256)
        tmp[...] = acc[:, source] + dot(e[:, :128], fa[:, source]) + dot(e[:, 128:], fb[:, source])
        for zl in range(4):
            rows = pl.ds(zl * 32, 32)
            own[rows, columns] = tmp[at(zl * 128 + y * 32, 32, 32), :]
            for k, out in ((1, s1), (2, s2), (3, s3)):
                out[rows, columns] = tmp[at(zl * 128 + (y + k) % 4 * 32, 32, 32), :].astype(BF16)
        return carry

    lax.fori_loop(0, 4, column, 0)


def grad_kernel(idx, w0, w1, w2, w3, d, l, fa, fb, r, keep, give, w):
    y, zl, c = idx[1], idx[2], idx[4]
    for k, block in enumerate((w0, w1, w2, w3)):
        jy = (y + 4 - k) % 4
        for back in range(4):
            jz = (zl + 4 - back) % 4
            w[at((jz * 4 + jy) * 32, 32, 32), :] = block[back * 32 : (back + 1) * 32, :]

    def column(j, carry):
        columns = at(j * 256, 256, 256)
        part = w[columns, :]
        for k, block in enumerate((d, l, None, r)):
            if block is None:
                p_a, p_b = dot(fa[...], part, 1), dot(fb[...], part, 1)
            else:
                p = dot(block[...], part, 1)
                p_a, p_b = p[:128], p[128:]
            keep[k, :, columns] = jnp.where(c == 0, p_a, p_b)
            give[k, :, columns] = jnp.where(c == 0, p_b, p_a)
        return carry

    lax.fori_loop(0, 2, column, 0)


def core_sum_kernel(idx, keep, got, own, give):
    zh = idx[3]
    mine, theirs = at(zh * 64, 64, 64), at((1 - zh) * 64, 64, 64)
    for k in range(keep.shape[0]):
        own[k] = keep[k, mine, :] + got[k, mine, :]
        give[k] = (keep[k, theirs, :] + got[k, theirs, :]).astype(BF16)


def half_sum_kernel(idx, own, got, *outs):
    for k, out in enumerate(outs):
        out[...] = own[k] + got[k].astype(F32)


def norm_backward_kernel(idx, h, gain, t0, t1, t2, t3, g, out):
    x, zh, c = idx[0], idx[3], idx[4]
    rows = at(c * 128 + zh * 64, 64, 64)
    h_all = h[rows, :].astype(F32)
    scale = jnp.sqrt(jnp.mean(h_all * h_all, axis=-1, keepdims=True) + epsilon)
    normed, scaled, total = [], [], 0.0
    for k, term in enumerate((t0, t1, t2, t3)):
        columns = at((x + k) % 4 * 512, 512, 512)
        normed.append(h[rows, columns].astype(F32) / scale)
        scaled.append(gain[:, columns] * term[...])
        total = total + jnp.sum(scaled[k] * normed[k], axis=-1, keepdims=True)
    mean = total / 2048
    for k in range(4):
        columns = at((x + k) % 4 * 512, 512, 512)
        out[:, columns] = ((scaled[k] - normed[k] * mean) / scale).astype(BF16)
    lane = lax.broadcasted_iota(jnp.int32, (32, 128), 1)
    high = g[...].astype(BF16).astype(F32)
    middle = (g[...] - high).astype(BF16).astype(F32)
    low = g[...] - high - middle
    out[:32, 2048:] = jnp.where(lane == 0, high, jnp.where(lane == 1, middle, jnp.where(lane == 2, low, 0.0))).astype(BF16)
    out[32:, 2048:] = jnp.zeros((32, 128), BF16)


def final_kernel(idx, divisor, own, across, own_c, across_c, out, gain_out):
    zh, c = idx[3], idx[4]
    for block, other_h, other_c in ((own, 0, 0), (across, 1, 0), (own_c, 0, 1), (across_c, 1, 1)):
        out[at(((c + other_c) % 2 * 2 + (zh + other_h) % 2) * 64, 64, 64), :] = block[:, :2048]

    def term(block):
        return jnp.sum(block[:32, 2048:].astype(F32), axis=-1, keepdims=True)

    total = (term(own) + term(own_c)) + (term(across) + term(across_c))
    gain_out[...] = jnp.broadcast_to(total, (32, 128)).T[:1, :] / divisor[...]


def y_sum_kernel(start, idx, own, g1, g2, g3, w, mine, g0, s1, s2, s3):
    zl = idx[2]
    lane = lax.broadcasted_iota(jnp.int32, (32, 128), 1)
    for k, out in enumerate((mine, s1, s2, s3)):
        rows = at((zl + k) % 4 * 32, 32, 32)
        total = own[rows, :] + g1[rows, :].astype(F32) + g2[rows, :].astype(F32) + g3[rows, :].astype(F32)
        back = (4 - k) % 4
        w_part = w[back * 32 : (back + 1) * 32, start : start + 1024].astype(F32)
        gain_term = jnp.sum(total * w_part, axis=-1, keepdims=True)
        if k == 0:
            mine[...] = total
            g0[...] = jnp.broadcast_to(gain_term, (32, 128))
        else:
            out[:, :1024] = total.astype(BF16)
            high = gain_term.astype(BF16).astype(F32)
            out[:, 1024:] = jnp.where(lane == 0, high, jnp.where(lane == 1, gain_term - high, 0.0)).astype(BF16)


def z_sum_kernel(idx, mine_a, g_a, a1, a2, a3, mine_b, g_b, b1, b2, b3, out, gain_out):
    total = g_a[...] + g_b[...]
    for start, mine, s1, s2, s3 in ((0, mine_a, a1, a2, a3), (1024, mine_b, b1, b2, b3)):
        part = mine[...] + s1[:, :1024].astype(F32) + s2[:, :1024].astype(F32) + s3[:, :1024].astype(F32)
        out[:, start : start + 1024] = part * (1.0 / 64)
        tail = s1[:, 1024:].astype(F32) + s2[:, 1024:].astype(F32) + s3[:, 1024:].astype(F32)
        total = total + jnp.sum(tail, axis=-1, keepdims=True)
    gain_out[...] = total


def program(hidden, gain, w_value, d_value):
    flat = lax.axis_index("dp") * 4 + lax.axis_index("pipe")
    idx = (flat // jnp.array([64, 4, 16, 2, 1])) % jnp.array([4, 4, 4, 2, 2])
    d, w = d_value[0], w_value[0]
    gain_row = gain.reshape(1, 2048)

    l, r = send(d, dx=1), send(d, dx=3)
    w1, w3, w2 = (send(w, dl=k) for k in (1, 3, 2))
    e_own, e1, e2, e3 = call(
        norm_kernel, [((512, 256), BF16)] + [((512, 128), BF16)] * 3, 3_000_000, idx, hidden, gain_row,
        scratch=[pltpu.VMEM((256, 128), F32)],
    )
    m1, m3, m2 = send(e1, dx=1), send(e3, dx=3), send(e2, dx=2)
    z_rows = jnp.concatenate([w, w1, w2, w3])
    y1, y3, y2 = (send(z_rows, dy=k) for k in (1, 3, 2))
    oth = send(jnp.stack([m1, m2, m3]), dc=1)
    l_half, r_half = l[:128], r[128:]
    fa, fb = send(l_half, dx=1), send(r_half, dx=3)

    (acc,) = call(
        value_near_kernel, [((512, 2048), F32)], 1_610_000_000, idx, e_own, m1, m3, oth, d, l, r,
        scratch=[pltpu.VMEM((512, 512), BF16)], mib=20,
    )
    keep, give = call(
        grad_kernel, [((4, 128, 512), F32)] * 2, 2_147_000_000, idx, z_rows, y1, y2, y3, d, l, fa, fb, r,
        scratch=[pltpu.VMEM((512, 2048), BF16)], mib=20,
    )
    got = send(give, dc=1)

    def far(start):
        return call(
            functools.partial(value_far_kernel, start), [((128, 1024), F32)] + [((128, 1024), BF16)] * 3,
            268_000_000, idx, m2, oth, acc, fa, fb,
            scratch=[pltpu.VMEM((512, 256), BF16), pltpu.VMEM((512, 256), F32)], mib=20,
        )

    def y_sum(start, v_own, v1, v2, v3):
        v1, v3, v2 = send(v1, dy=1), send(v3, dy=3), send(v2, dy=2)
        mine, g0, s1, s2, s3 = call(
            functools.partial(y_sum_kernel, start),
            [((32, 1024), F32), ((32, 128), F32)] + [((32, 1152), BF16)] * 3, 1_000_000, idx, v_own, v1, v2, v3, z_rows,
        )
        return mine, g0, send(s1, dl=1), send(s2, dl=2), send(s3, dl=3)

    parts = []
    for start in (0, 1024):
        parts.extend(y_sum(start, *far(start)))

    own, give = call(core_sum_kernel, [((4, 64, 512), F32), ((4, 64, 512), BF16)], 1_000_000, idx, keep, got)
    got = send(give, dh=1)
    t0, t1, t2, t3 = call(half_sum_kernel, [((64, 512), F32)] * 4, 1_000_000, idx, own, got)
    t1, t3, t2 = send(t1, dx=3), send(t3, dx=1), send(t2, dx=2)
    grad_value, g = call(z_sum_kernel, [((32, 2048), F32), ((32, 128), F32)], 1_000_000, idx, *parts)
    (result,) = call(norm_backward_kernel, [((64, 2176), BF16)], 1_000_000, idx, hidden, gain_row, t0, t1, t2, t3, g)
    across, result_c = send(result, dh=1), send(result, dc=1)
    across_c = send(across, dc=1)
    divisor = 64 * lax.dynamic_slice(gain_row, (0, flat // 4 * 32), (1, 32))
    grad_hidden, g = call(
        final_kernel, [((256, 2048), BF16), ((1, 32), F32)], 1_000_000,
        idx, divisor, result, across, result_c, across_c,
    )
    grad_gain = g.reshape(32)
    return (grad_hidden, grad_gain, grad_value[None])


def solution(mesh):
    return jax.shard_map(
        program,
        mesh=mesh,
        in_specs=(P("dp", None), P(), P("pipe", "dp", None), P("pipe", "dp", None)),
        out_specs=(P("dp", None), P("dp"), P("pipe", "dp", None)),
        check_vma=False,
    )
```

time: 148 us -> 136 us (0.919)
  the two profiles are of different devices: /device:TPU:41 before, /device:TPU:1 now
where the time goes in v2:
time: 136 us
  starting transfers between devices  59.6 us (44%)
  waiting for transfers between devices  47.6 us (35%)
  Pallas kernels  21.4 us (16%)
  local copies, waits for them, and re-layouts  4.83 us (4%)
  other arithmetic  1.98 us (1%)
    ppermute x34, starting transfers between devices, send(): return lax.ppermute(value, AXES, pairs(**shift))  59.6 us
    ppermute x34, waiting for transfers between devices, send(): return lax.ppermute(value, AXES, pairs(**shift))  47.6 us
    pallas_call x12, Pallas kernels, call(): pl.pallas_call(body, out_shape=shapes, in_specs=[SMEM] + [VMEM] * (len(ar...  21.4 us
    unnamed x12, local copies, waits for them, and re-layouts  3.16 us
  transfers between devices with their start and end apart: 34, of which 12 were waited for; matrix products, arithmetic and copies ran while one was open for 3% of the time, Pallas kernels for 14%

profile of v2, /device:TPU:1, one launch (start us, length us, event | category | flops | bytes accessed | tf_op | source)
XLA Modules:
  0.0 136.1 jit_solution(16203327089179946521)
XLA Ops:
  0.6 2.1 %collective-permute-start.6 = (bf16[256,2048]{1,0:T(8,128)(2,1)}, bf16[256,2048]{1,0:T(8,128)(2,1)S(1)}, u32[]{:S(2)}, u32[]{:S(2)}) collective-permute-start(bf16[256,2048]{1,0:T(8,128)(2,1)} %bitcast.11), channel_id=1, source_target_pairs={{0,64},{1,65},{2,66},{3,67},{4,68},{5,69},{6,70},{7,71},{8,72},{9,... | collective-permute-start | bytes 3145736 | tf_op jit(solution)/shard_map/ppermute | solution.py:32
  4.1 4.4 %collective-permute-start.2 = (bf16[32,2048]{1,0:T(8,128)(2,1)}, bf16[32,2048]{1,0:T(8,128)(2,1)S(1)}, u32[]{:S(2)}, u32[]{:S(2)}) collective-permute-start(bf16[32,2048]{1,0:T(8,128)(2,1)} %bitcast.19), channel_id=1, source_target_pairs={{0,48},{1,49},{2,50},{3,51},{4,52},{5,53},{6,54},{7,55},{8,56},{9,... | collective-permute-start | bytes 393224 | tf_op jit(solution)/shard_map/ppermute | solution.py:32
  8.8 2.0 %collective-permute-done.2 = bf16[32,2048]{1,0:T(8,128)(2,1)S(1)} collective-permute-done((bf16[32,2048]{1,0:T(8,128)(2,1)}, bf16[32,2048]{1,0:T(8,128)(2,1)S(1)}, u32[]{:S(2)}, u32[]{:S(2)}) %collective-permute-start.2) | collective-permute-done | bytes 131104 | tf_op jit(solution)/shard_map/ppermute | solution.py:32
  10.8 8.4 %collective-permute-done.1 = bf16[32,2048]{1,0:T(8,128)(2,1)S(1)} collective-permute-done((bf16[32,2048]{1,0:T(8,128)(2,1)}, bf16[32,2048]{1,0:T(8,128)(2,1)S(1)}, u32[]{:S(2)}, u32[]{:S(2)}) %collective-permute-start.1) | collective-permute-done | bytes 131104 | tf_op jit(solution)/shard_map/ppermute | solution.py:32
  21.6 2.6 %collective-permute-start.4 = (bf16[128,2048]{1,0:T(8,128)(2,1)S(1)}, bf16[128,2048]{1,0:T(8,128)(2,1)}, u32[]{:S(2)}, u32[]{:S(2)}) collective-permute-start(bf16[128,2048]{1,0:T(8,128)(2,1)S(1)} %pad_maximum_fusion.w0.w), channel_id=1, source_target_pairs={{0,8},{1,9},{2,10},{3,11},{4,12},{5,13},{6,14},{7,15},{8,0},{9,1},... | collective-permute-start | bytes 1572872 | tf_op jit(solution)/shard_map/ppermute | solution.py:32
  26.1 1.6 %collective-permute-start.7 = (bf16[128,2048]{1,0:T(8,128)(2,1)}, bf16[128,2048]{1,0:T(8,128)(2,1)S(1)}, u32[]{:S(2)}, u32[]{:S(2)}) collective-permute-start(bf16[128,2048]{1,0:T(8,128)(2,1)} %slice.8), channel_id=1, source_target_pairs={{0,64},{1,65},{2,66},{3,67},{4,68},{5,69},{6,70},{7,71},{8,72},{9,... | collective-permute-start | bytes 1572872 | tf_op jit(solution)/shard_map/ppermute | solution.py:32
  34.1 1.8 %collective-permute-start.15 = (bf16[512,128]{1,0:T(8,128)(2,1)S(1)}, bf16[512,128]{1,0:T(8,128)(2,1)S(1)}, u32[]{:S(2)}, u32[]{:S(2)}) collective-permute-start(bf16[512,128]{1,0:T(8,128)(2,1)S(1)} %get-tuple-element.45), channel_id=1, source_target_pairs={{0,128},{1,129},{2,130},{3,131},{4,132},{5,133},{6,134},{7,135},{8... | collective-permute-start | bytes 393224 | tf_op jit(solution)/shard_map/ppermute | solution.py:32
  35.9 10.3 %collective-permute-done.4.w2 = bf16[128,2048]{1,0:T(8,128)(2,1)} collective-permute-done((bf16[128,2048]{1,0:T(8,128)(2,1)S(1)}, bf16[128,2048]{1,0:T(8,128)(2,1)}, u32[]{:S(2)}, u32[]{:S(2)}) %collective-permute-start.4) | collective-permute-done | bytes 524320 | tf_op jit(solution)/shard_map/ppermute | solution.py:32
  48.9 5.0 %shard_map.85 = (f32[4,128,512]{2,1,0:T(8,128)S(1)}, f32[4,128,512]{2,1,0:T(8,128)S(1)}) custom-call(s32[5]{0:T(128)S(1)} %and_select_fusion.idx, bf16[128,2048]{1,0:T(8,128)(2,1)S(1)} %pad_maximum_fusion.w0.w, bf16[128,2048]{1,0:T(8,128)(2,1)} %collective-permute-done.3.w1, bf16[128,2048]{1,0:T(8,128)(2,1)} %collective-permute-done.4.w2, ...), custom_call_target="tpu_custom_call" | custom-call | flops 2147000064 | bytes 8388628 | tf_op jit(solution)/shard_map/pallas_call | solution.py:38
  53.9 3.1 %collective-permute-start.10 = (f32[4,128,512]{2,1,0:T(8,128)S(1)}, f32[4,128,512]{2,1,0:T(8,128)S(1)}, u32[]{:S(2)}, u32[]{:S(2)}) collective-permute-start(f32[4,128,512]{2,1,0:T(8,128)S(1)} %get-tuple-element.38), channel_id=1, source_target_pairs={{0,1},{1,0},{2,3},{3,2},{4,5},{5,4},{6,7},{7,6},{8,9},{9,8},{10,11... | collective-permute-start | bytes 3145736 | tf_op jit(solution)/shard_map/ppermute | solution.py:32
  57.1 2.7 %collective-permute-done.18.oth = bf16[3,512,128]{2,1,0:T(8,128)(2,1)S(1)} collective-permute-done((bf16[3,512,128]{2,1,0:T(8,128)(2,1)S(1)}, bf16[3,512,128]{2,1,0:T(8,128)(2,1)S(1)}, u32[]{:S(2)}, u32[]{:S(2)}) %collective-permute-start.18) | collective-permute-done | bytes 393248 | tf_op jit(solution)/shard_map/ppermute | solution.py:32
  59.8 3.7 %shard_map.89.acc = f32[512,2048]{1,0:T(8,128)S(1)} custom-call(s32[5]{0:T(128)S(1)} %and_select_fusion.idx, bf16[512,256]{1,0:T(8,128)(2,1)S(1)} %get-tuple-element.48.e_own, bf16[512,128]{1,0:T(8,128)(2,1)S(1)} %collective-permute-done.16.m1, bf16[512,128]{1,0:T(8,128)(2,1)S(1)} %collective-permute-done.17.m3, ...), custom_call_target="tpu_custom_call" | custom-call | flops 1610000000 | bytes 8257556 | tf_op jit(solution)/shard_map/pallas_call | solution.py:38
  63.5 2.4 %shard_map.90 = (f32[128,1024]{1,0:T(8,128)S(1)}, bf16[128,1024]{1,0:T(8,128)(2,1)S(1)}, bf16[128,1024]{1,0:T(8,128)(2,1)S(1)}, bf16[128,1024]{1,0:T(8,128)(2,1)S(1)}) custom-call(s32[5]{0:T(128)S(1)} %and_select_fusion.idx, bf16[512,128]{1,0:T(8,128)(2,1)S(1)} %collective-permute-done.15.m2, bf16[3,512,128]{2,1,0:T(8,128)(2,1)S(1)} %collective-permute-done.18.oth, ...), custom_call_target="tpu_custom_call" | custom-call | flops 268000000 | bytes 7077908 | tf_op jit(solution)/shard_map/pallas_call | solution.py:38
  66.0 2.4 %collective-permute-start.20 = (bf16[128,1024]{1,0:T(8,128)(2,1)S(1)}, bf16[128,1024]{1,0:T(8,128)(2,1)S(1)}, u32[]{:S(2)}, u32[]{:S(2)}) collective-permute-start(bf16[128,1024]{1,0:T(8,128)(2,1)S(1)} %get-tuple-element.51), channel_id=1, source_target_pairs={{0,8},{1,9},{2,10},{3,11},{4,12},{5,13},{6,14},{7,15},{8,0},{9,1},... | collective-permute-start | bytes 786440 | tf_op jit(solution)/shard_map/ppermute | solution.py:32
  68.4 2.0 %collective-permute-start.21 = (bf16[128,1024]{1,0:T(8,128)(2,1)S(1)}, bf16[128,1024]{1,0:T(8,128)(2,1)S(1)}, u32[]{:S(2)}, u32[]{:S(2)}) collective-permute-start(bf16[128,1024]{1,0:T(8,128)(2,1)S(1)} %get-tuple-element.52), channel_id=1, source_target_pairs={{0,12},{1,13},{2,14},{3,15},{4,0},{5,1},{6,2},{7,3},{8,4},{9,5},{1... | collective-permute-start | bytes 786440 | tf_op jit(solution)/shard_map/ppermute | solution.py:32
  70.3 2.4 %shard_map.92 = (f32[128,1024]{1,0:T(8,128)S(1)}, bf16[128,1024]{1,0:T(8,128)(2,1)S(1)}, bf16[128,1024]{1,0:T(8,128)(2,1)S(1)}, bf16[128,1024]{1,0:T(8,128)(2,1)S(1)}) custom-call(s32[5]{0:T(128)S(1)} %and_select_fusion.idx, bf16[512,128]{1,0:T(8,128)(2,1)S(1)} %collective-permute-done.15.m2, bf16[3,512,128]{2,1,0:T(8,128)(2,1)S(1)} %collective-permute-done.18.oth, ...), custom_call_target="tpu_custom_call" | custom-call | flops 268000000 | bytes 7077908 | tf_op jit(solution)/shard_map/pallas_call | solution.py:38
  72.9 1.9 %collective-permute-done.19.g1 = bf16[128,1024]{1,0:T(8,128)(2,1)S(1)} collective-permute-done((bf16[128,1024]{1,0:T(8,128)(2,1)S(1)}, bf16[128,1024]{1,0:T(8,128)(2,1)S(1)}, u32[]{:S(2)}, u32[]{:S(2)}) %collective-permute-start.19) | collective-permute-done | bytes 262176 | tf_op jit(solution)/shard_map/ppermute | solution.py:32
  76.9 3.4 %collective-permute-done.20.g2 = bf16[128,1024]{1,0:T(8,128)(2,1)S(1)} collective-permute-done((bf16[128,1024]{1,0:T(8,128)(2,1)S(1)}, bf16[128,1024]{1,0:T(8,128)(2,1)S(1)}, u32[]{:S(2)}, u32[]{:S(2)}) %collective-permute-start.20) | collective-permute-done | bytes 262176 | tf_op jit(solution)/shard_map/ppermute | solution.py:32
  80.2 5.9 %collective-permute-start.11 = (bf16[4,64,512]{2,1,0:T(8,128)(2,1)S(1)}, bf16[4,64,512]{2,1,0:T(8,128)(2,1)S(1)}, u32[]{:S(2)}, u32[]{:S(2)}) collective-permute-start(bf16[4,64,512]{2,1,0:T(8,128)(2,1)S(1)} %get-tuple-element.40), channel_id=1, source_target_pairs={{0,2},{1,3},{2,0},{3,1},{4,6},{5,7},{6,4},{7,5},{8,10},{9,11},{10,... | collective-permute-start | bytes 786440 | tf_op jit(solution)/shard_map/ppermute | solution.py:32
  87.7 1.9 %collective-permute-start.23 = (bf16[32,1152]{1,0:T(8,128)(2,1)S(1)}, bf16[32,1152]{1,0:T(8,128)(2,1)S(1)}, u32[]{:S(2)}, u32[]{:S(2)}) collective-permute-start(bf16[32,1152]{1,0:T(8,128)(2,1)S(1)} %get-tuple-element.56), channel_id=1, source_target_pairs={{0,32},{1,33},{2,34},{3,35},{4,36},{5,37},{6,38},{7,39},{8,40},{9,... | collective-permute-start | bytes 221192 | tf_op jit(solution)/shard_map/ppermute | solution.py:32
  89.6 1.9 %collective-permute-done.26.g2 = bf16[128,1024]{1,0:T(8,128)(2,1)S(1)} collective-permute-done((bf16[128,1024]{1,0:T(8,128)(2,1)S(1)}, bf16[128,1024]{1,0:T(8,128)(2,1)S(1)}, u32[]{:S(2)}, u32[]{:S(2)}) %collective-permute-start.26) | collective-permute-done | bytes 262176 | tf_op jit(solution)/shard_map/ppermute | solution.py:32
  91.5 3.3 %collective-permute-start.24 = (bf16[32,1152]{1,0:T(8,128)(2,1)S(1)}, bf16[32,1152]{1,0:T(8,128)(2,1)S(1)}, u32[]{:S(2)}, u32[]{:S(2)}) collective-permute-start(bf16[32,1152]{1,0:T(8,128)(2,1)S(1)} %get-tuple-element.57), channel_id=1, source_target_pairs={{0,48},{1,49},{2,50},{3,51},{4,52},{5,53},{6,54},{7,55},{8,56},{9,... | collective-permute-start | bytes 221192 | tf_op jit(solution)/shard_map/ppermute | solution.py:32
  96.3 3.5 %collective-permute-start.12 = (f32[64,512]{1,0:T(8,128)S(1)}, f32[64,512]{1,0:T(8,128)S(1)}, u32[]{:S(2)}, u32[]{:S(2)}) collective-permute-start(f32[64,512]{1,0:T(8,128)S(1)} %get-tuple-element.42), channel_id=1, source_target_pairs={{0,192},{1,193},{2,194},{3,195},{4,196},{5,197},{6,198},{7,199},{8... | collective-permute-start | bytes 393224 | tf_op jit(solution)/shard_map/ppermute | solution.py:32
  99.8 4.9 %collective-permute-done.23.a2 = bf16[32,1152]{1,0:T(8,128)(2,1)S(1)} collective-permute-done((bf16[32,1152]{1,0:T(8,128)(2,1)S(1)}, bf16[32,1152]{1,0:T(8,128)(2,1)S(1)}, u32[]{:S(2)}, u32[]{:S(2)}) %collective-permute-start.23) | collective-permute-done | bytes 73760 | tf_op jit(solution)/shard_map/ppermute | solution.py:32
  104.7 2.5 %collective-permute-start.29 = (bf16[32,1152]{1,0:T(8,128)(2,1)S(1)}, bf16[32,1152]{1,0:T(8,128)(2,1)S(1)}, u32[]{:S(2)}, u32[]{:S(2)}) collective-permute-start(bf16[32,1152]{1,0:T(8,128)(2,1)S(1)} %get-tuple-element.65), channel_id=1, source_target_pairs={{0,32},{1,33},{2,34},{3,35},{4,36},{5,37},{6,38},{7,39},{8,40},{9,... | collective-permute-start | bytes 221192 | tf_op jit(solution)/shard_map/ppermute | solution.py:32
  107.2 2.2 %collective-permute-start.30 = (bf16[32,1152]{1,0:T(8,128)(2,1)S(1)}, bf16[32,1152]{1,0:T(8,128)(2,1)S(1)}, u32[]{:S(2)}, u32[]{:S(2)}) collective-permute-start(bf16[32,1152]{1,0:T(8,128)(2,1)S(1)} %get-tuple-element.66), channel_id=1, source_target_pairs={{0,48},{1,49},{2,50},{3,51},{4,52},{5,53},{6,54},{7,55},{8,56},{9,... | collective-permute-start | bytes 221192 | tf_op jit(solution)/shard_map/ppermute | solution.py:32
  109.4 1.9 %collective-permute-done.30.b3 = bf16[32,1152]{1,0:T(8,128)(2,1)S(1)} collective-permute-done((bf16[32,1152]{1,0:T(8,128)(2,1)S(1)}, bf16[32,1152]{1,0:T(8,128)(2,1)S(1)}, u32[]{:S(2)}, u32[]{:S(2)}) %collective-permute-start.30) | collective-permute-done | bytes 73760 | tf_op jit(solution)/shard_map/ppermute | solution.py:32
  114.2 1.8 %collective-permute-start.31 = (bf16[64,2176]{1,0:T(8,128)(2,1)S(1)}, bf16[64,2176]{1,0:T(8,128)(2,1)S(1)}, u32[]{:S(2)}, u32[]{:S(2)}) collective-permute-start(bf16[64,2176]{1,0:T(8,128)(2,1)S(1)} %shard_map.95.own), channel_id=1, source_target_pairs={{0,2},{1,3},{2,0},{3,1},{4,6},{5,7},{6,4},{7,5},{8,10},{9,11},{10,... | collective-permute-start | bytes 835592 | tf_op jit(solution)/shard_map/ppermute | solution.py:32
  116.0 5.2 %collective-permute-start.32 = (bf16[64,2176]{1,0:T(8,128)(2,1)S(1)}, bf16[64,2176]{1,0:T(8,128)(2,1)S(1)}, u32[]{:S(2)}, u32[]{:S(2)}) collective-permute-start(bf16[64,2176]{1,0:T(8,128)(2,1)S(1)} %shard_map.95.own), channel_id=1, source_target_pairs={{0,1},{1,0},{2,3},{3,2},{4,5},{5,4},{6,7},{7,6},{8,9},{9,8},{10,11... | collective-permute-start | bytes 835592 | tf_op jit(solution)/shard_map/ppermute | solution.py:32
  121.2 8.4 %collective-permute-done.31.across = bf16[64,2176]{1,0:T(8,128)(2,1)S(1)} collective-permute-done((bf16[64,2176]{1,0:T(8,128)(2,1)S(1)}, bf16[64,2176]{1,0:T(8,128)(2,1)S(1)}, u32[]{:S(2)}, u32[]{:S(2)}) %collective-permute-start.31) | collective-permute-done | bytes 278560 | tf_op jit(solution)/shard_map/ppermute | solution.py:32
  129.6 3.7 %collective-permute-start.33 = (bf16[64,2176]{1,0:T(8,128)(2,1)S(1)}, bf16[64,2176]{1,0:T(8,128)(2,1)S(1)}, u32[]{:S(2)}, u32[]{:S(2)}) collective-permute-start(bf16[64,2176]{1,0:T(8,128)(2,1)S(1)} %collective-permute-done.31.across), channel_id=1, source_target_pairs={{0,1},{1,0},{2,3},{3,2},{4,5},{5,4},{6,7},{7,6},{8,9},{9,8},{10,11... | collective-permute-start | bytes 835592 | tf_op jit(solution)/shard_map/ppermute | solution.py:32
  134.5 1.7 %shard_map.96 = (bf16[256,2048]{1,0:T(8,128)(2,1)}, f32[1,32]{1,0:T(1,128)}) custom-call(s32[5]{0:T(128)S(1)} %and_select_fusion.idx, f32[1,32]{1,0:T(1,128)S(1)} %multiply_bitcast_fusion.divisor, bf16[64,2176]{1,0:T(8,128)(2,1)S(1)} %shard_map.95.own, bf16[64,2176]{1,0:T(8,128)(2,1)S(1)} %collective-permute-done.31.across, ...), custom_call_target="tpu_custom_call" | custom-call | flops 1000000 | bytes 2162964 | tf_op jit(solution)/shard_map/pallas_call | solution.py:38
  (66 shorter events, 24.5 us)
Async XLA Ops:
  0.6 24.6 %collective-permute-start.6 = (bf16[256,2048]{1,0:T(8,128)(2,1)}, bf16[256,2048]{1,0:T(8,128)(2,1)S(1)}, u32[]{:S(2)}, u32[]{:S(2)}) collective-permute-start(bf16[256,2048]{1,0:T(8,128)(2,1)} %bitcast.11), channel_id=1, source_target_pairs={{0,64},{1,65},{2,66},{3,67},{4,68},{5,69},{6,70},{7,71},{8,72},{9,... | collective-permute-start | bytes 3145736 | tf_op jit(solution)/shard_map/ppermute | solution.py:32
  2.7 25.0 %collective-permute-start.8 = (bf16[256,2048]{1,0:T(8,128)(2,1)}, bf16[256,2048]{1,0:T(8,128)(2,1)S(1)}, u32[]{:S(2)}, u32[]{:S(2)}) collective-permute-start(bf16[256,2048]{1,0:T(8,128)(2,1)} %bitcast.12), channel_id=1, source_target_pairs={{0,192},{1,193},{2,194},{3,195},{4,196},{5,197},{6,198},{7,199},{8... | collective-permute-start | bytes 3145736 | tf_op jit(solution)/shard_map/ppermute | solution.py:32
  4.1 6.7 %collective-permute-start.2 = (bf16[32,2048]{1,0:T(8,128)(2,1)}, bf16[32,2048]{1,0:T(8,128)(2,1)S(1)}, u32[]{:S(2)}, u32[]{:S(2)}) collective-permute-start(bf16[32,2048]{1,0:T(8,128)(2,1)} %bitcast.19), channel_id=1, source_target_pairs={{0,48},{1,49},{2,50},{3,51},{4,52},{5,53},{6,54},{7,55},{8,56},{9,... | collective-permute-start | bytes 393224 | tf_op jit(solution)/shard_map/ppermute | solution.py:32
  8.5 10.7 %collective-permute-start.1 = (bf16[32,2048]{1,0:T(8,128)(2,1)}, bf16[32,2048]{1,0:T(8,128)(2,1)S(1)}, u32[]{:S(2)}, u32[]{:S(2)}) collective-permute-start(bf16[32,2048]{1,0:T(8,128)(2,1)} %bitcast.20), channel_id=1, source_target_pairs={{0,32},{1,33},{2,34},{3,35},{4,36},{5,37},{6,38},{7,39},{8,40},{9,... | collective-permute-start | bytes 393224 | tf_op jit(solution)/shard_map/ppermute | solution.py:32
  8.6 10.7 %collective-permute-start = (bf16[32,2048]{1,0:T(8,128)(2,1)}, bf16[32,2048]{1,0:T(8,128)(2,1)S(1)}, u32[]{:S(2)}, u32[]{:S(2)}) collective-permute-start(bf16[32,2048]{1,0:T(8,128)(2,1)} %bitcast.21), channel_id=1, source_target_pairs={{0,16},{1,17},{2,18},{3,19},{4,20},{5,21},{6,22},{7,23},{8,24},{9,... | collective-permute-start | bytes 393224 | tf_op jit(solution)/shard_map/ppermute | solution.py:32
  20.2 13.9 %collective-permute-start.3 = (bf16[128,2048]{1,0:T(8,128)(2,1)S(1)}, bf16[128,2048]{1,0:T(8,128)(2,1)}, u32[]{:S(2)}, u32[]{:S(2)}) collective-permute-start(bf16[128,2048]{1,0:T(8,128)(2,1)S(1)} %pad_maximum_fusion.w0.w), channel_id=1, source_target_pairs={{0,4},{1,5},{2,6},{3,7},{4,8},{5,9},{6,10},{7,11},{8,12},{9,13},{1... | collective-permute-start | bytes 1572872 | tf_op jit(solution)/shard_map/ppermute | solution.py:32
  21.6 24.6 %collective-permute-start.4 = (bf16[128,2048]{1,0:T(8,128)(2,1)S(1)}, bf16[128,2048]{1,0:T(8,128)(2,1)}, u32[]{:S(2)}, u32[]{:S(2)}) collective-permute-start(bf16[128,2048]{1,0:T(8,128)(2,1)S(1)} %pad_maximum_fusion.w0.w), channel_id=1, source_target_pairs={{0,8},{1,9},{2,10},{3,11},{4,12},{5,13},{6,14},{7,15},{8,0},{9,1},... | collective-permute-start | bytes 1572872 | tf_op jit(solution)/shard_map/ppermute | solution.py:32
  24.2 23.2 %collective-permute-start.5 = (bf16[128,2048]{1,0:T(8,128)(2,1)S(1)}, bf16[128,2048]{1,0:T(8,128)(2,1)}, u32[]{:S(2)}, u32[]{:S(2)}) collective-permute-start(bf16[128,2048]{1,0:T(8,128)(2,1)S(1)} %pad_maximum_fusion.w0.w), channel_id=1, source_target_pairs={{0,12},{1,13},{2,14},{3,15},{4,0},{5,1},{6,2},{7,3},{8,4},{9,5},{1... | collective-permute-start | bytes 1572872 | tf_op jit(solution)/shard_map/ppermute | solution.py:32
  26.1 21.5 %collective-permute-start.7 = (bf16[128,2048]{1,0:T(8,128)(2,1)}, bf16[128,2048]{1,0:T(8,128)(2,1)S(1)}, u32[]{:S(2)}, u32[]{:S(2)}) collective-permute-start(bf16[128,2048]{1,0:T(8,128)(2,1)} %slice.8), channel_id=1, source_target_pairs={{0,64},{1,65},{2,66},{3,67},{4,68},{5,69},{6,70},{7,71},{8,72},{9,... | collective-permute-start | bytes 1572872 | tf_op jit(solution)/shard_map/ppermute | solution.py:32
  28.5 19.1 %collective-permute-start.9 = (bf16[128,2048]{1,0:T(8,128)(2,1)}, bf16[128,2048]{1,0:T(8,128)(2,1)}, u32[]{:S(2)}, u32[]{:S(2)}) collective-permute-start(bf16[128,2048]{1,0:T(8,128)(2,1)} %slice.9), channel_id=1, source_target_pairs={{0,192},{1,193},{2,194},{3,195},{4,196},{5,197},{6,198},{7,199},{8... | collective-permute-start | bytes 1572872 | tf_op jit(solution)/shard_map/ppermute | solution.py:32
  34.1 22.9 %collective-permute-start.15 = (bf16[512,128]{1,0:T(8,128)(2,1)S(1)}, bf16[512,128]{1,0:T(8,128)(2,1)S(1)}, u32[]{:S(2)}, u32[]{:S(2)}) collective-permute-start(bf16[512,128]{1,0:T(8,128)(2,1)S(1)} %get-tuple-element.45), channel_id=1, source_target_pairs={{0,128},{1,129},{2,130},{3,131},{4,132},{5,133},{6,134},{7,135},{8... | collective-permute-start | bytes 393224 | tf_op jit(solution)/shard_map/ppermute | solution.py:32
  46.2 10.8 %collective-permute-start.17 = (bf16[512,128]{1,0:T(8,128)(2,1)S(1)}, bf16[512,128]{1,0:T(8,128)(2,1)S(1)}, u32[]{:S(2)}, u32[]{:S(2)}) collective-permute-start(bf16[512,128]{1,0:T(8,128)(2,1)S(1)} %get-tuple-element.47), channel_id=1, source_target_pairs={{0,192},{1,193},{2,194},{3,195},{4,196},{5,197},{6,198},{7,199},{8... | collective-permute-start | bytes 393224 | tf_op jit(solution)/shard_map/ppermute | solution.py:32
  47.5 9.5 %collective-permute-start.16 = (bf16[512,128]{1,0:T(8,128)(2,1)S(1)}, bf16[512,128]{1,0:T(8,128)(2,1)S(1)}, u32[]{:S(2)}, u32[]{:S(2)}) collective-permute-start(bf16[512,128]{1,0:T(8,128)(2,1)S(1)} %get-tuple-element.46), channel_id=1, source_target_pairs={{0,64},{1,65},{2,66},{3,67},{4,68},{5,69},{6,70},{7,71},{8,72},{9,... | collective-permute-start | bytes 393224 | tf_op jit(solution)/shard_map/ppermute | solution.py:32
  53.9 22.4 %collective-permute-start.10 = (f32[4,128,512]{2,1,0:T(8,128)S(1)}, f32[4,128,512]{2,1,0:T(8,128)S(1)}, u32[]{:S(2)}, u32[]{:S(2)}) collective-permute-start(f32[4,128,512]{2,1,0:T(8,128)S(1)} %get-tuple-element.38), channel_id=1, source_target_pairs={{0,1},{1,0},{2,3},{3,2},{4,5},{5,4},{6,7},{7,6},{8,9},{9,8},{10,11... | collective-permute-start | bytes 3145736 | tf_op jit(solution)/shard_map/ppermute | solution.py:32
  65.9 8.9 %collective-permute-start.19 = (bf16[128,1024]{1,0:T(8,128)(2,1)S(1)}, bf16[128,1024]{1,0:T(8,128)(2,1)S(1)}, u32[]{:S(2)}, u32[]{:S(2)}) collective-permute-start(bf16[128,1024]{1,0:T(8,128)(2,1)S(1)} %get-tuple-element.50), channel_id=1, source_target_pairs={{0,4},{1,5},{2,6},{3,7},{4,8},{5,9},{6,10},{7,11},{8,12},{9,13},{1... | collective-permute-start | bytes 786440 | tf_op jit(solution)/shard_map/ppermute | solution.py:32
  66.0 14.2 %collective-permute-start.20 = (bf16[128,1024]{1,0:T(8,128)(2,1)S(1)}, bf16[128,1024]{1,0:T(8,128)(2,1)S(1)}, u32[]{:S(2)}, u32[]{:S(2)}) collective-permute-start(bf16[128,1024]{1,0:T(8,128)(2,1)S(1)} %get-tuple-element.51), channel_id=1, source_target_pairs={{0,8},{1,9},{2,10},{3,11},{4,12},{5,13},{6,14},{7,15},{8,0},{9,1},... | collective-permute-start | bytes 786440 | tf_op jit(solution)/shard_map/ppermute | solution.py:32
  68.4 17.8 %collective-permute-start.21 = (bf16[128,1024]{1,0:T(8,128)(2,1)S(1)}, bf16[128,1024]{1,0:T(8,128)(2,1)S(1)}, u32[]{:S(2)}, u32[]{:S(2)}) collective-permute-start(bf16[128,1024]{1,0:T(8,128)(2,1)S(1)} %get-tuple-element.52), channel_id=1, source_target_pairs={{0,12},{1,13},{2,14},{3,15},{4,0},{5,1},{6,2},{7,3},{8,4},{9,5},{1... | collective-permute-start | bytes 786440 | tf_op jit(solution)/shard_map/ppermute | solution.py:32
  72.8 14.9 %collective-permute-start.25 = (bf16[128,1024]{1,0:T(8,128)(2,1)S(1)}, bf16[128,1024]{1,0:T(8,128)(2,1)S(1)}, u32[]{:S(2)}, u32[]{:S(2)}) collective-permute-start(bf16[128,1024]{1,0:T(8,128)(2,1)S(1)} %get-tuple-element.59), channel_id=1, source_target_pairs={{0,4},{1,5},{2,6},{3,7},{4,8},{5,9},{6,10},{7,11},{8,12},{9,13},{1... | collective-permute-start | bytes 786440 | tf_op jit(solution)/shard_map/ppermute | solution.py:32
  74.8 16.7 %collective-permute-start.26 = (bf16[128,1024]{1,0:T(8,128)(2,1)S(1)}, bf16[128,1024]{1,0:T(8,128)(2,1)S(1)}, u32[]{:S(2)}, u32[]{:S(2)}) collective-permute-start(bf16[128,1024]{1,0:T(8,128)(2,1)S(1)} %get-tuple-element.60), channel_id=1, source_target_pairs={{0,8},{1,9},{2,10},{3,11},{4,12},{5,13},{6,14},{7,15},{8,0},{9,1},... | collective-permute-start | bytes 786440 | tf_op jit(solution)/shard_map/ppermute | solution.py:32
  76.2 18.6 %collective-permute-start.27 = (bf16[128,1024]{1,0:T(8,128)(2,1)S(1)}, bf16[128,1024]{1,0:T(8,128)(2,1)S(1)}, u32[]{:S(2)}, u32[]{:S(2)}) collective-permute-start(bf16[128,1024]{1,0:T(8,128)(2,1)S(1)} %get-tuple-element.61), channel_id=1, source_target_pairs={{0,12},{1,13},{2,14},{3,15},{4,0},{5,1},{6,2},{7,3},{8,4},{9,5},{1... | collective-permute-start | bytes 786440 | tf_op jit(solution)/shard_map/ppermute | solution.py:32
  80.2 15.5 %collective-permute-start.11 = (bf16[4,64,512]{2,1,0:T(8,128)(2,1)S(1)}, bf16[4,64,512]{2,1,0:T(8,128)(2,1)S(1)}, u32[]{:S(2)}, u32[]{:S(2)}) collective-permute-start(bf16[4,64,512]{2,1,0:T(8,128)(2,1)S(1)} %get-tuple-element.40), channel_id=1, source_target_pairs={{0,2},{1,3},{2,0},{3,1},{4,6},{5,7},{6,4},{7,5},{8,10},{9,11},{10,... | collective-permute-start | bytes 786440 | tf_op jit(solution)/shard_map/ppermute | solution.py:32
  87.0 12.8 %collective-permute-start.22 = (bf16[32,1152]{1,0:T(8,128)(2,1)S(1)}, bf16[32,1152]{1,0:T(8,128)(2,1)S(1)}, u32[]{:S(2)}, u32[]{:S(2)}) collective-permute-start(bf16[32,1152]{1,0:T(8,128)(2,1)S(1)} %get-tuple-element.55), channel_id=1, source_target_pairs={{0,16},{1,17},{2,18},{3,19},{4,20},{5,21},{6,22},{7,23},{8,24},{9,... | collective-permute-start | bytes 221192 | tf_op jit(solution)/shard_map/ppermute | solution.py:32
  87.7 16.9 %collective-permute-start.23 = (bf16[32,1152]{1,0:T(8,128)(2,1)S(1)}, bf16[32,1152]{1,0:T(8,128)(2,1)S(1)}, u32[]{:S(2)}, u32[]{:S(2)}) collective-permute-start(bf16[32,1152]{1,0:T(8,128)(2,1)S(1)} %get-tuple-element.56), channel_id=1, source_target_pairs={{0,32},{1,33},{2,34},{3,35},{4,36},{5,37},{6,38},{7,39},{8,40},{9,... | collective-permute-start | bytes 221192 | tf_op jit(solution)/shard_map/ppermute | solution.py:32
  91.5 13.1 %collective-permute-start.24 = (bf16[32,1152]{1,0:T(8,128)(2,1)S(1)}, bf16[32,1152]{1,0:T(8,128)(2,1)S(1)}, u32[]{:S(2)}, u32[]{:S(2)}) collective-permute-start(bf16[32,1152]{1,0:T(8,128)(2,1)S(1)} %get-tuple-element.57), channel_id=1, source_target_pairs={{0,48},{1,49},{2,50},{3,51},{4,52},{5,53},{6,54},{7,55},{8,56},{9,... | collective-permute-start | bytes 221192 | tf_op jit(solution)/shard_map/ppermute | solution.py:32
  95.6 11.6 %collective-permute-start.28 = (bf16[32,1152]{1,0:T(8,128)(2,1)S(1)}, bf16[32,1152]{1,0:T(8,128)(2,1)S(1)}, u32[]{:S(2)}, u32[]{:S(2)}) collective-permute-start(bf16[32,1152]{1,0:T(8,128)(2,1)S(1)} %get-tuple-element.64), channel_id=1, source_target_pairs={{0,16},{1,17},{2,18},{3,19},{4,20},{5,21},{6,22},{7,23},{8,24},{9,... | collective-permute-start | bytes 221192 | tf_op jit(solution)/shard_map/ppermute | solution.py:32
  96.3 16.3 %collective-permute-start.12 = (f32[64,512]{1,0:T(8,128)S(1)}, f32[64,512]{1,0:T(8,128)S(1)}, u32[]{:S(2)}, u32[]{:S(2)}) collective-permute-start(f32[64,512]{1,0:T(8,128)S(1)} %get-tuple-element.42), channel_id=1, source_target_pairs={{0,192},{1,193},{2,194},{3,195},{4,196},{5,197},{6,198},{7,199},{8... | collective-permute-start | bytes 393224 | tf_op jit(solution)/shard_map/ppermute | solution.py:32
  99.8 12.8 %collective-permute-start.13 = (f32[64,512]{1,0:T(8,128)S(1)}, f32[64,512]{1,0:T(8,128)S(1)}, u32[]{:S(2)}, u32[]{:S(2)}) collective-permute-start(f32[64,512]{1,0:T(8,128)S(1)} %get-tuple-element.43), channel_id=1, source_target_pairs={{0,128},{1,129},{2,130},{3,131},{4,132},{5,133},{6,134},{7,135},{8... | collective-permute-start | bytes 393224 | tf_op jit(solution)/shard_map/ppermute | solution.py:32
  104.7 8.6 %collective-permute-start.14 = (f32[64,512]{1,0:T(8,128)S(1)}, f32[64,512]{1,0:T(8,128)S(1)}, u32[]{:S(2)}, u32[]{:S(2)}) collective-permute-start(f32[64,512]{1,0:T(8,128)S(1)} %get-tuple-element.44), channel_id=1, source_target_pairs={{0,64},{1,65},{2,66},{3,67},{4,68},{5,69},{6,70},{7,71},{8,72},{9,... | collective-permute-start | bytes 393224 | tf_op jit(solution)/shard_map/ppermute | solution.py:32
  104.7 4.7 %collective-permute-start.29 = (bf16[32,1152]{1,0:T(8,128)(2,1)S(1)}, bf16[32,1152]{1,0:T(8,128)(2,1)S(1)}, u32[]{:S(2)}, u32[]{:S(2)}) collective-permute-start(bf16[32,1152]{1,0:T(8,128)(2,1)S(1)} %get-tuple-element.65), channel_id=1, source_target_pairs={{0,32},{1,33},{2,34},{3,35},{4,36},{5,37},{6,38},{7,39},{8,40},{9,... | collective-permute-start | bytes 221192 | tf_op jit(solution)/shard_map/ppermute | solution.py:32
  114.2 15.4 %collective-permute-start.31 = (bf16[64,2176]{1,0:T(8,128)(2,1)S(1)}, bf16[64,2176]{1,0:T(8,128)(2,1)S(1)}, u32[]{:S(2)}, u32[]{:S(2)}) collective-permute-start(bf16[64,2176]{1,0:T(8,128)(2,1)S(1)} %shard_map.95.own), channel_id=1, source_target_pairs={{0,2},{1,3},{2,0},{3,1},{4,6},{5,7},{6,4},{7,5},{8,10},{9,11},{10,... | collective-permute-start | bytes 835592 | tf_op jit(solution)/shard_map/ppermute | solution.py:32
  116.0 17.4 %collective-permute-start.32 = (bf16[64,2176]{1,0:T(8,128)(2,1)S(1)}, bf16[64,2176]{1,0:T(8,128)(2,1)S(1)}, u32[]{:S(2)}, u32[]{:S(2)}) collective-permute-start(bf16[64,2176]{1,0:T(8,128)(2,1)S(1)} %shard_map.95.own), channel_id=1, source_target_pairs={{0,1},{1,0},{2,3},{3,2},{4,5},{5,4},{6,7},{7,6},{8,9},{9,8},{10,11... | collective-permute-start | bytes 835592 | tf_op jit(solution)/shard_map/ppermute | solution.py:32
  129.6 4.9 %collective-permute-start.33 = (bf16[64,2176]{1,0:T(8,128)(2,1)S(1)}, bf16[64,2176]{1,0:T(8,128)(2,1)S(1)}, u32[]{:S(2)}, u32[]{:S(2)}) collective-permute-start(bf16[64,2176]{1,0:T(8,128)(2,1)S(1)} %collective-permute-done.31.across), channel_id=1, source_target_pairs={{0,1},{1,0},{2,3},{3,2},{4,5},{5,4},{6,7},{7,6},{8,9},{9,8},{10,11... | collective-permute-start | bytes 835592 | tf_op jit(solution)/shard_map/ppermute | solution.py:32
  (8 other events, 102.0 us)

commit v3 on v2

--- a/solution.py
+++ b/solution.py
@@ -87,7 +87,7 @@
 
     def column(j, carry):
         columns, source = at(j * 256, 256, 256), at(start + j * 256, 256, 256)
-        tmp[...] = acc[:, source] + dot(e[:, :128], fa[:, source]) + dot(e[:, 128:], fb[:, source])
+        tmp[...] = acc[:, source] + dot(e[:, :128], fa[:, columns]) + dot(e[:, 128:], fb[:, columns])
         for zl in range(4):
             rows = pl.ds(zl * 32, 32)
             own[rows, columns] = tmp[at(zl * 128 + y * 32, 32, 32), :]
@@ -98,7 +98,7 @@
     lax.fori_loop(0, 4, column, 0)
 
 
-def grad_kernel(idx, w0, w1, w2, w3, d, l, fa, fb, r, keep, give, w):
+def grad_kernel(idx, w0, w1, w2, w3, d, l, fa0, fb0, fa1, fb1, r, keep, give, w):
     y, zl, c = idx[1], idx[2], idx[4]
     for k, block in enumerate((w0, w1, w2, w3)):
         jy = (y + 4 - k) % 4
@@ -111,7 +111,8 @@
         part = w[columns, :]
         for k, block in enumerate((d, l, None, r)):
             if block is None:
-                p_a, p_b = dot(fa[...], part, 1), dot(fb[...], part, 1)
+                p_a = dot(fa0[...], part[:, :1024], 1) + dot(fa1[...], part[:, 1024:], 1)
+                p_b = dot(fb0[...], part[:, :1024], 1) + dot(fb1[...], part[:, 1024:], 1)
             else:
                 p = dot(block[...], part, 1)
                 p_a, p_b = p[:128], p[128:]
@@ -214,15 +215,17 @@
     z_rows = jnp.concatenate([w, w1, w2, w3])
     y1, y3, y2 = (send(z_rows, dy=k) for k in (1, 3, 2))
     oth = send(jnp.stack([m1, m2, m3]), dc=1)
-    l_half, r_half = l[:128], r[128:]
-    fa, fb = send(l_half, dx=1), send(r_half, dx=3)
+    l_halves = [l[:128, at : at + 1024] for at in (0, 1024)]
+    r_halves = [r[128:, at : at + 1024] for at in (0, 1024)]
+    fa0, fb0 = send(l_halves[0], dx=1), send(r_halves[0], dx=3)
+    fa1, fb1 = send(l_halves[1], dx=1), send(r_halves[1], dx=3)
 
     (acc,) = call(
         value_near_kernel, [((512, 2048), F32)], 1_610_000_000, idx, e_own, m1, m3, oth, d, l, r,
         scratch=[pltpu.VMEM((512, 512), BF16)], mib=20,
     )
     keep, give = call(
-        grad_kernel, [((4, 128, 512), F32)] * 2, 2_147_000_000, idx, z_rows, y1, y2, y3, d, l, fa, fb, r,
+        grad_kernel, [((4, 128, 512), F32)] * 2, 2_147_000_000, idx, z_rows, y1, y2, y3, d, l, fa0, fb0, fa1, fb1, r,
         scratch=[pltpu.VMEM((512, 2048), BF16)], mib=20,
     )
     got = send(give, dc=1)
@@ -230,7 +233,7 @@
     def far(start):
         return call(
             functools.partial(value_far_kernel, start), [((128, 1024), F32)] + [((128, 1024), BF16)] * 3,
-            268_000_000, idx, m2, oth, acc, fa, fb,
+            268_000_000, idx, m2, oth, acc, *((fa0, fb0) if start == 0 else (fa1, fb1)),
             scratch=[pltpu.VMEM((512, 256), BF16), pltpu.VMEM((512, 256), F32)], mib=20,
         )
 

time: 136 us -> 151 us (1.11)
  the two profiles are of different devices: /device:TPU:1 before, /device:TPU:33 now
where the time goes in v3:
time: 151 us
  waiting for transfers between devices  63 us (42%)
  starting transfers between devices  56.4 us (37%)
  Pallas kernels  20.3 us (13%)
  local copies, waits for them, and re-layouts  8.48 us (6%)
  other arithmetic  1.98 us (1%)
    ppermute x36, waiting for transfers between devices, send(): return lax.ppermute(value, AXES, pairs(**shift))  63 us
    ppermute x36, starting transfers between devices, send(): return lax.ppermute(value, AXES, pairs(**shift))  56.4 us
    pallas_call x12, Pallas kernels, call(): pl.pallas_call(body, out_shape=shapes, in_specs=[SMEM] + [VMEM] * (len(ar...  20.3 us
    unnamed x18, local copies, waits for them, and re-layouts  6.82 us
  transfers between devices with their start and end apart: 36, of which 15 were waited for; matrix products, arithmetic and copies ran while one was open for 2% of the time, Pallas kernels for 12%

profile of v3, /device:TPU:33, one launch (start us, length us, event | category | flops | bytes accessed | tf_op | source)
XLA Modules:
  0.0 150.9 jit_solution(12394201966937714234)
XLA Ops:
  0.6 2.6 %collective-permute-start.8 = (bf16[256,2048]{1,0:T(8,128)(2,1)}, bf16[256,2048]{1,0:T(8,128)(2,1)S(1)}, u32[]{:S(2)}, u32[]{:S(2)}) collective-permute-start(bf16[256,2048]{1,0:T(8,128)(2,1)} %bitcast.11), channel_id=1, source_target_pairs={{0,192},{1,193},{2,194},{3,195},{4,196},{5,197},{6,198},{7,199},{8... | collective-permute-start | bytes 3145736 | tf_op jit(solution)/shard_map/ppermute | solution.py:32
  3.2 3.0 %collective-permute-start.1 = (bf16[32,2048]{1,0:T(8,128)(2,1)}, bf16[32,2048]{1,0:T(8,128)(2,1)S(1)}, u32[]{:S(2)}, u32[]{:S(2)}) collective-permute-start(bf16[32,2048]{1,0:T(8,128)(2,1)} %bitcast.20), channel_id=1, source_target_pairs={{0,32},{1,33},{2,34},{3,35},{4,36},{5,37},{6,38},{7,39},{8,40},{9,... | collective-permute-start | bytes 393224 | tf_op jit(solution)/shard_map/ppermute | solution.py:32
  6.2 2.4 %collective-permute-start = (bf16[32,2048]{1,0:T(8,128)(2,1)}, bf16[32,2048]{1,0:T(8,128)(2,1)S(1)}, u32[]{:S(2)}, u32[]{:S(2)}) collective-permute-start(bf16[32,2048]{1,0:T(8,128)(2,1)} %bitcast.21), channel_id=1, source_target_pairs={{0,16},{1,17},{2,18},{3,19},{4,20},{5,21},{6,22},{7,23},{8,24},{9,... | collective-permute-start | bytes 393224 | tf_op jit(solution)/shard_map/ppermute | solution.py:32
  8.5 4.9 %collective-permute-done.1 = bf16[32,2048]{1,0:T(8,128)(2,1)S(1)} collective-permute-done((bf16[32,2048]{1,0:T(8,128)(2,1)}, bf16[32,2048]{1,0:T(8,128)(2,1)S(1)}, u32[]{:S(2)}, u32[]{:S(2)}) %collective-permute-start.1) | collective-permute-done | bytes 131104 | tf_op jit(solution)/shard_map/ppermute | solution.py:32
  13.4 3.8 %collective-permute-done = bf16[32,2048]{1,0:T(8,128)(2,1)S(1)} collective-permute-done((bf16[32,2048]{1,0:T(8,128)(2,1)}, bf16[32,2048]{1,0:T(8,128)(2,1)S(1)}, u32[]{:S(2)}, u32[]{:S(2)}) %collective-permute-start) | collective-permute-done | bytes 131104 | tf_op jit(solution)/shard_map/ppermute | solution.py:32
  18.2 2.8 %collective-permute-start.5 = (bf16[128,2048]{1,0:T(8,128)(2,1)S(1)}, bf16[128,2048]{1,0:T(8,128)(2,1)S(1)}, u32[]{:S(2)}, u32[]{:S(2)}) collective-permute-start(bf16[128,2048]{1,0:T(8,128)(2,1)S(1)} %pad_maximum_fusion.w0.w), channel_id=1, source_target_pairs={{0,12},{1,13},{2,14},{3,15},{4,0},{5,1},{6,2},{7,3},{8,4},{9,5},{1... | collective-permute-start | bytes 1572872 | tf_op jit(solution)/shard_map/ppermute | solution.py:32
  22.0 3.3 %collective-permute-done.8.r = bf16[256,2048]{1,0:T(8,128)(2,1)S(1)} collective-permute-done((bf16[256,2048]{1,0:T(8,128)(2,1)}, bf16[256,2048]{1,0:T(8,128)(2,1)S(1)}, u32[]{:S(2)}, u32[]{:S(2)}) %collective-permute-start.8) | collective-permute-done | bytes 1048608 | tf_op jit(solution)/shard_map/ppermute | solution.py:32
  26.2 3.3 %collective-permute-start.11 = (bf16[128,1024]{1,0:T(8,128)(2,1)}, bf16[128,1024]{1,0:T(8,128)(2,1)S(1)}, u32[]{:S(2)}, u32[]{:S(2)}) collective-permute-start(bf16[128,1024]{1,0:T(8,128)(2,1)} %get-tuple-element.71), channel_id=1, source_target_pairs={{0,192},{1,193},{2,194},{3,195},{4,196},{5,197},{6,198},{7,199},{8... | collective-permute-start | bytes 786440 | tf_op jit(solution)/shard_map/ppermute | solution.py:32
  30.3 1.6 %collective-permute-done.5.w3 = bf16[128,2048]{1,0:T(8,128)(2,1)S(1)} collective-permute-done((bf16[128,2048]{1,0:T(8,128)(2,1)S(1)}, bf16[128,2048]{1,0:T(8,128)(2,1)S(1)}, u32[]{:S(2)}, u32[]{:S(2)}) %collective-permute-start.5) | collective-permute-done | bytes 524320 | tf_op jit(solution)/shard_map/ppermute | solution.py:32
  32.9 1.5 collective-permute-done.4.w2
  39.4 8.3 %collective-permute-done.3.w1 = bf16[128,2048]{1,0:T(8,128)(2,1)} collective-permute-done((bf16[128,2048]{1,0:T(8,128)(2,1)S(1)}, bf16[128,2048]{1,0:T(8,128)(2,1)}, u32[]{:S(2)}, u32[]{:S(2)}) %collective-permute-start.3) | collective-permute-done | bytes 524320 | tf_op jit(solution)/shard_map/ppermute | solution.py:32
  47.7 1.7 %collective-permute-start.17 = (bf16[512,128]{1,0:T(8,128)(2,1)S(1)}, bf16[512,128]{1,0:T(8,128)(2,1)S(1)}, u32[]{:S(2)}, u32[]{:S(2)}) collective-permute-start(bf16[512,128]{1,0:T(8,128)(2,1)S(1)} %get-tuple-element.45), channel_id=1, source_target_pairs={{0,128},{1,129},{2,130},{3,131},{4,132},{5,133},{6,134},{7,135},{8... | collective-permute-start | bytes 393224 | tf_op jit(solution)/shard_map/ppermute | solution.py:32
  49.4 1.5 %collective-permute-start.18 = (bf16[512,128]{1,0:T(8,128)(2,1)S(1)}, bf16[512,128]{1,0:T(8,128)(2,1)S(1)}, u32[]{:S(2)}, u32[]{:S(2)}) collective-permute-start(bf16[512,128]{1,0:T(8,128)(2,1)S(1)} %get-tuple-element.46), channel_id=1, source_target_pairs={{0,64},{1,65},{2,66},{3,67},{4,68},{5,69},{6,70},{7,71},{8,72},{9,... | collective-permute-start | bytes 393224 | tf_op jit(solution)/shard_map/ppermute | solution.py:32
  55.4 4.5 %shard_map.85 = (f32[4,128,512]{2,1,0:T(8,128)S(1)}, f32[4,128,512]{2,1,0:T(8,128)S(1)}) custom-call(s32[5]{0:T(128)S(1)} %and_select_fusion.idx, bf16[128,2048]{1,0:T(8,128)(2,1)S(1)} %pad_maximum_fusion.w0.w, bf16[128,2048]{1,0:T(8,128)(2,1)} %collective-permute-done.3.w1, bf16[128,2048]{1,0:T(8,128)(2,1)S(1)} %copy-done.8, ...), custom_call_target="tpu_custom_call" | custom-call | flops 2147000064 | bytes 8388628 | tf_op jit(solution)/shard_map/pallas_call | solution.py:38
  60.0 6.5 %collective-permute-start.12 = (f32[4,128,512]{2,1,0:T(8,128)S(1)}, f32[4,128,512]{2,1,0:T(8,128)S(1)}, u32[]{:S(2)}, u32[]{:S(2)}) collective-permute-start(f32[4,128,512]{2,1,0:T(8,128)S(1)} %get-tuple-element.38), channel_id=1, source_target_pairs={{0,1},{1,0},{2,3},{3,2},{4,5},{5,4},{6,7},{7,6},{8,9},{9,8},{10,11... | collective-permute-start | bytes 3145736 | tf_op jit(solution)/shard_map/ppermute | solution.py:32
  66.7 2.7 %collective-permute-done.20.oth = bf16[3,512,128]{2,1,0:T(8,128)(2,1)S(1)} collective-permute-done((bf16[3,512,128]{2,1,0:T(8,128)(2,1)S(1)}, bf16[3,512,128]{2,1,0:T(8,128)(2,1)S(1)}, u32[]{:S(2)}, u32[]{:S(2)}) %collective-permute-start.20) | collective-permute-done | bytes 393248 | tf_op jit(solution)/shard_map/ppermute | solution.py:32
  69.4 3.7 %shard_map.89.acc = f32[512,2048]{1,0:T(8,128)S(1)} custom-call(s32[5]{0:T(128)S(1)} %and_select_fusion.idx, bf16[512,256]{1,0:T(8,128)(2,1)S(1)} %get-tuple-element.48.e_own, bf16[512,128]{1,0:T(8,128)(2,1)S(1)} %collective-permute-done.18.m1, bf16[512,128]{1,0:T(8,128)(2,1)S(1)} %collective-permute-done.19.m3, ...), custom_call_target="tpu_custom_call" | custom-call | flops 1610000000 | bytes 8257556 | tf_op jit(solution)/shard_map/pallas_call | solution.py:38
  73.1 2.3 %shard_map.92 = (f32[128,1024]{1,0:T(8,128)S(1)}, bf16[128,1024]{1,0:T(8,128)(2,1)S(1)}, bf16[128,1024]{1,0:T(8,128)(2,1)S(1)}, bf16[128,1024]{1,0:T(8,128)(2,1)S(1)}) custom-call(s32[5]{0:T(128)S(1)} %and_select_fusion.idx, bf16[512,128]{1,0:T(8,128)(2,1)S(1)} %collective-permute-done.17.m2, bf16[3,512,128]{2,1,0:T(8,128)(2,1)S(1)} %collective-permute-done.20.oth, ...), custom_call_target="tpu_custom_call" | custom-call | flops 268000000 | bytes 6553620 | tf_op jit(solution)/shard_map/pallas_call | solution.py:38
  75.6 4.4 %collective-permute-start.28 = (bf16[128,1024]{1,0:T(8,128)(2,1)S(1)}, bf16[128,1024]{1,0:T(8,128)(2,1)S(1)}, u32[]{:S(2)}, u32[]{:S(2)}) collective-permute-start(bf16[128,1024]{1,0:T(8,128)(2,1)S(1)} %get-tuple-element.60), channel_id=1, source_target_pairs={{0,8},{1,9},{2,10},{3,11},{4,12},{5,13},{6,14},{7,15},{8,0},{9,1},... | collective-permute-start | bytes 786440 | tf_op jit(solution)/shard_map/ppermute | solution.py:32
  80.1 1.9 %shard_map.90 = (f32[128,1024]{1,0:T(8,128)S(1)}, bf16[128,1024]{1,0:T(8,128)(2,1)S(1)}, bf16[128,1024]{1,0:T(8,128)(2,1)S(1)}, bf16[128,1024]{1,0:T(8,128)(2,1)S(1)}) custom-call(s32[5]{0:T(128)S(1)} %and_select_fusion.idx, bf16[512,128]{1,0:T(8,128)(2,1)S(1)} %collective-permute-done.17.m2, bf16[3,512,128]{2,1,0:T(8,128)(2,1)S(1)} %collective-permute-done.20.oth, ...), custom_call_target="tpu_custom_call" | custom-call | flops 268000000 | bytes 6553620 | tf_op jit(solution)/shard_map/pallas_call | solution.py:38
  82.0 1.5 %collective-permute-start.21 = (bf16[128,1024]{1,0:T(8,128)(2,1)S(1)}, bf16[128,1024]{1,0:T(8,128)(2,1)S(1)}, u32[]{:S(2)}, u32[]{:S(2)}) collective-permute-start(bf16[128,1024]{1,0:T(8,128)(2,1)S(1)} %get-tuple-element.50), channel_id=1, source_target_pairs={{0,4},{1,5},{2,6},{3,7},{4,8},{5,9},{6,10},{7,11},{8,12},{9,13},{1... | collective-permute-start | bytes 786440 | tf_op jit(solution)/shard_map/ppermute | solution.py:32
  83.5 1.7 %collective-permute-done.27.g1 = bf16[128,1024]{1,0:T(8,128)(2,1)S(1)} collective-permute-done((bf16[128,1024]{1,0:T(8,128)(2,1)S(1)}, bf16[128,1024]{1,0:T(8,128)(2,1)S(1)}, u32[]{:S(2)}, u32[]{:S(2)}) %collective-permute-start.27) | collective-permute-done | bytes 262176 | tf_op jit(solution)/shard_map/ppermute | solution.py:32
  87.0 4.7 %collective-permute-done.28.g2 = bf16[128,1024]{1,0:T(8,128)(2,1)S(1)} collective-permute-done((bf16[128,1024]{1,0:T(8,128)(2,1)S(1)}, bf16[128,1024]{1,0:T(8,128)(2,1)S(1)}, u32[]{:S(2)}, u32[]{:S(2)}) %collective-permute-start.28) | collective-permute-done | bytes 262176 | tf_op jit(solution)/shard_map/ppermute | solution.py:32
  91.7 9.3 %collective-permute-start.13 = (bf16[4,64,512]{2,1,0:T(8,128)(2,1)S(1)}, bf16[4,64,512]{2,1,0:T(8,128)(2,1)S(1)}, u32[]{:S(2)}, u32[]{:S(2)}) collective-permute-start(bf16[4,64,512]{2,1,0:T(8,128)(2,1)S(1)} %get-tuple-element.40), channel_id=1, source_target_pairs={{0,2},{1,3},{2,0},{3,1},{4,6},{5,7},{6,4},{7,5},{8,10},{9,11},{10,... | collective-permute-start | bytes 786440 | tf_op jit(solution)/shard_map/ppermute | solution.py:32
  101.8 2.1 %collective-permute-start.30 = (bf16[32,1152]{1,0:T(8,128)(2,1)S(1)}, bf16[32,1152]{1,0:T(8,128)(2,1)S(1)}, u32[]{:S(2)}, u32[]{:S(2)}) collective-permute-start(bf16[32,1152]{1,0:T(8,128)(2,1)S(1)} %get-tuple-element.64), channel_id=1, source_target_pairs={{0,16},{1,17},{2,18},{3,19},{4,20},{5,21},{6,22},{7,23},{8,24},{9,... | collective-permute-start | bytes 221192 | tf_op jit(solution)/shard_map/ppermute | solution.py:32
  106.4 9.8 %collective-permute-done.13.got = bf16[4,64,512]{2,1,0:T(8,128)(2,1)S(1)} collective-permute-done((bf16[4,64,512]{2,1,0:T(8,128)(2,1)S(1)}, bf16[4,64,512]{2,1,0:T(8,128)(2,1)S(1)}, u32[]{:S(2)}, u32[]{:S(2)}) %collective-permute-start.13) | collective-permute-done | bytes 262176 | tf_op jit(solution)/shard_map/ppermute | solution.py:32
  119.1 2.2 %collective-permute-done.32.b3 = bf16[32,1152]{1,0:T(8,128)(2,1)S(1)} collective-permute-done((bf16[32,1152]{1,0:T(8,128)(2,1)S(1)}, bf16[32,1152]{1,0:T(8,128)(2,1)S(1)}, u32[]{:S(2)}, u32[]{:S(2)}) %collective-permute-start.32) | collective-permute-done | bytes 73760 | tf_op jit(solution)/shard_map/ppermute | solution.py:32
  121.7 3.9 %collective-permute-done.25.a2 = bf16[32,1152]{1,0:T(8,128)(2,1)S(1)} collective-permute-done((bf16[32,1152]{1,0:T(8,128)(2,1)S(1)}, bf16[32,1152]{1,0:T(8,128)(2,1)S(1)}, u32[]{:S(2)}, u32[]{:S(2)}) %collective-permute-start.25) | collective-permute-done | bytes 73760 | tf_op jit(solution)/shard_map/ppermute | solution.py:32
  129.1 4.0 %collective-permute-start.33 = (bf16[64,2176]{1,0:T(8,128)(2,1)S(1)}, bf16[64,2176]{1,0:T(8,128)(2,1)S(1)}, u32[]{:S(2)}, u32[]{:S(2)}) collective-permute-start(bf16[64,2176]{1,0:T(8,128)(2,1)S(1)} %shard_map.95.own), channel_id=1, source_target_pairs={{0,2},{1,3},{2,0},{3,1},{4,6},{5,7},{6,4},{7,5},{8,10},{9,11},{10,... | collective-permute-start | bytes 835592 | tf_op jit(solution)/shard_map/ppermute | solution.py:32
  133.8 12.3 %collective-permute-done.33.across = bf16[64,2176]{1,0:T(8,128)(2,1)S(1)} collective-permute-done((bf16[64,2176]{1,0:T(8,128)(2,1)S(1)}, bf16[64,2176]{1,0:T(8,128)(2,1)S(1)}, u32[]{:S(2)}, u32[]{:S(2)}) %collective-permute-start.33) | collective-permute-done | bytes 278560 | tf_op jit(solution)/shard_map/ppermute | solution.py:32
  146.1 2.0 %collective-permute-start.35 = (bf16[64,2176]{1,0:T(8,128)(2,1)S(1)}, bf16[64,2176]{1,0:T(8,128)(2,1)S(1)}, u32[]{:S(2)}, u32[]{:S(2)}) collective-permute-start(bf16[64,2176]{1,0:T(8,128)(2,1)S(1)} %collective-permute-done.33.across), channel_id=1, source_target_pairs={{0,1},{1,0},{2,3},{3,2},{4,5},{5,4},{6,7},{7,6},{8,9},{9,8},{10,11... | collective-permute-start | bytes 835592 | tf_op jit(solution)/shard_map/ppermute | solution.py:32
  149.3 1.7 %shard_map.96 = (bf16[256,2048]{1,0:T(8,128)(2,1)}, f32[1,32]{1,0:T(1,128)}) custom-call(s32[5]{0:T(128)S(1)} %and_select_fusion.idx, f32[1,32]{1,0:T(1,128)S(1)} %multiply_bitcast_fusion.divisor, bf16[64,2176]{1,0:T(8,128)(2,1)S(1)} %shard_map.95.own, bf16[64,2176]{1,0:T(8,128)(2,1)S(1)} %collective-permute-done.33.across, ...), custom_call_target="tpu_custom_call" | custom-call | flops 1000000 | bytes 2162964 | tf_op jit(solution)/shard_map/pallas_call | solution.py:38
  (76 shorter events, 28.3 us)
Async XLA Ops:
  0.6 24.7 %collective-permute-start.8 = (bf16[256,2048]{1,0:T(8,128)(2,1)}, bf16[256,2048]{1,0:T(8,128)(2,1)S(1)}, u32[]{:S(2)}, u32[]{:S(2)}) collective-permute-start(bf16[256,2048]{1,0:T(8,128)(2,1)} %bitcast.11), channel_id=1, source_target_pairs={{0,192},{1,193},{2,194},{3,195},{4,196},{5,197},{6,198},{7,199},{8... | collective-permute-start | bytes 3145736 | tf_op jit(solution)/shard_map/ppermute | solution.py:32
  3.2 26.3 %collective-permute-start.6 = (bf16[256,2048]{1,0:T(8,128)(2,1)}, bf16[256,2048]{1,0:T(8,128)(2,1)S(1)}, u32[]{:S(2)}, u32[]{:S(2)}) collective-permute-start(bf16[256,2048]{1,0:T(8,128)(2,1)} %bitcast.12), channel_id=1, source_target_pairs={{0,64},{1,65},{2,66},{3,67},{4,68},{5,69},{6,70},{7,71},{8,72},{9,... | collective-permute-start | bytes 3145736 | tf_op jit(solution)/shard_map/ppermute | solution.py:32
  3.2 10.2 %collective-permute-start.1 = (bf16[32,2048]{1,0:T(8,128)(2,1)}, bf16[32,2048]{1,0:T(8,128)(2,1)S(1)}, u32[]{:S(2)}, u32[]{:S(2)}) collective-permute-start(bf16[32,2048]{1,0:T(8,128)(2,1)} %bitcast.20), channel_id=1, source_target_pairs={{0,32},{1,33},{2,34},{3,35},{4,36},{5,37},{6,38},{7,39},{8,40},{9,... | collective-permute-start | bytes 393224 | tf_op jit(solution)/shard_map/ppermute | solution.py:32
  6.2 11.1 %collective-permute-start = (bf16[32,2048]{1,0:T(8,128)(2,1)}, bf16[32,2048]{1,0:T(8,128)(2,1)S(1)}, u32[]{:S(2)}, u32[]{:S(2)}) collective-permute-start(bf16[32,2048]{1,0:T(8,128)(2,1)} %bitcast.21), channel_id=1, source_target_pairs={{0,16},{1,17},{2,18},{3,19},{4,20},{5,21},{6,22},{7,23},{8,24},{9,... | collective-permute-start | bytes 393224 | tf_op jit(solution)/shard_map/ppermute | solution.py:32
  18.2 13.7 %collective-permute-start.5 = (bf16[128,2048]{1,0:T(8,128)(2,1)S(1)}, bf16[128,2048]{1,0:T(8,128)(2,1)S(1)}, u32[]{:S(2)}, u32[]{:S(2)}) collective-permute-start(bf16[128,2048]{1,0:T(8,128)(2,1)S(1)} %pad_maximum_fusion.w0.w), channel_id=1, source_target_pairs={{0,12},{1,13},{2,14},{3,15},{4,0},{5,1},{6,2},{7,3},{8,4},{9,5},{1... | collective-permute-start | bytes 1572872 | tf_op jit(solution)/shard_map/ppermute | solution.py:32
  21.0 13.4 %collective-permute-start.4 = (bf16[128,2048]{1,0:T(8,128)(2,1)S(1)}, bf16[128,2048]{1,0:T(8,128)(2,1)S(1)}, u32[]{:S(2)}, u32[]{:S(2)}) collective-permute-start(bf16[128,2048]{1,0:T(8,128)(2,1)S(1)} %pad_maximum_fusion.w0.w), channel_id=1, source_target_pairs={{0,8},{1,9},{2,10},{3,11},{4,12},{5,13},{6,14},{7,15},{8,0},{9,1},... | collective-permute-start | bytes 1572872 | tf_op jit(solution)/shard_map/ppermute | solution.py:32
  21.3 26.3 %collective-permute-start.3 = (bf16[128,2048]{1,0:T(8,128)(2,1)S(1)}, bf16[128,2048]{1,0:T(8,128)(2,1)}, u32[]{:S(2)}, u32[]{:S(2)}) collective-permute-start(bf16[128,2048]{1,0:T(8,128)(2,1)S(1)} %pad_maximum_fusion.w0.w), channel_id=1, source_target_pairs={{0,4},{1,5},{2,6},{3,7},{4,8},{5,9},{6,10},{7,11},{8,12},{9,13},{1... | collective-permute-start | bytes 1572872 | tf_op jit(solution)/shard_map/ppermute | solution.py:32
  26.2 23.2 %collective-permute-start.11 = (bf16[128,1024]{1,0:T(8,128)(2,1)}, bf16[128,1024]{1,0:T(8,128)(2,1)S(1)}, u32[]{:S(2)}, u32[]{:S(2)}) collective-permute-start(bf16[128,1024]{1,0:T(8,128)(2,1)} %get-tuple-element.71), channel_id=1, source_target_pairs={{0,192},{1,193},{2,194},{3,195},{4,196},{5,197},{6,198},{7,199},{8... | collective-permute-start | bytes 786440 | tf_op jit(solution)/shard_map/ppermute | solution.py:32
  29.5 21.5 %collective-permute-start.9 = (bf16[128,1024]{1,0:T(8,128)(2,1)}, bf16[128,1024]{1,0:T(8,128)(2,1)S(1)}, u32[]{:S(2)}, u32[]{:S(2)}) collective-permute-start(bf16[128,1024]{1,0:T(8,128)(2,1)} %get-tuple-element.72), channel_id=1, source_target_pairs={{0,192},{1,193},{2,194},{3,195},{4,196},{5,197},{6,198},{7,199},{8... | collective-permute-start | bytes 786440 | tf_op jit(solution)/shard_map/ppermute | solution.py:32
  32.7 19.4 %collective-permute-start.10 = (bf16[128,1024]{1,0:T(8,128)(2,1)}, bf16[128,1024]{1,0:T(8,128)(2,1)}, u32[]{:S(2)}, u32[]{:S(2)}) collective-permute-start(bf16[128,1024]{1,0:T(8,128)(2,1)} %get-tuple-element.73), channel_id=1, source_target_pairs={{0,64},{1,65},{2,66},{3,67},{4,68},{5,69},{6,70},{7,71},{8,72},{9,... | collective-permute-start | bytes 786440 | tf_op jit(solution)/shard_map/ppermute | solution.py:32
  35.2 16.9 %collective-permute-start.7 = (bf16[128,1024]{1,0:T(8,128)(2,1)}, bf16[128,1024]{1,0:T(8,128)(2,1)S(1)}, u32[]{:S(2)}, u32[]{:S(2)}) collective-permute-start(bf16[128,1024]{1,0:T(8,128)(2,1)} %get-tuple-element.74), channel_id=1, source_target_pairs={{0,64},{1,65},{2,66},{3,67},{4,68},{5,69},{6,70},{7,71},{8,72},{9,... | collective-permute-start | bytes 786440 | tf_op jit(solution)/shard_map/ppermute | solution.py:32
  47.7 18.8 %collective-permute-start.17 = (bf16[512,128]{1,0:T(8,128)(2,1)S(1)}, bf16[512,128]{1,0:T(8,128)(2,1)S(1)}, u32[]{:S(2)}, u32[]{:S(2)}) collective-permute-start(bf16[512,128]{1,0:T(8,128)(2,1)S(1)} %get-tuple-element.45), channel_id=1, source_target_pairs={{0,128},{1,129},{2,130},{3,131},{4,132},{5,133},{6,134},{7,135},{8... | collective-permute-start | bytes 393224 | tf_op jit(solution)/shard_map/ppermute | solution.py:32
  49.4 17.1 %collective-permute-start.18 = (bf16[512,128]{1,0:T(8,128)(2,1)S(1)}, bf16[512,128]{1,0:T(8,128)(2,1)S(1)}, u32[]{:S(2)}, u32[]{:S(2)}) collective-permute-start(bf16[512,128]{1,0:T(8,128)(2,1)S(1)} %get-tuple-element.46), channel_id=1, source_target_pairs={{0,64},{1,65},{2,66},{3,67},{4,68},{5,69},{6,70},{7,71},{8,72},{9,... | collective-permute-start | bytes 393224 | tf_op jit(solution)/shard_map/ppermute | solution.py:32
  50.9 15.6 %collective-permute-start.19 = (bf16[512,128]{1,0:T(8,128)(2,1)S(1)}, bf16[512,128]{1,0:T(8,128)(2,1)S(1)}, u32[]{:S(2)}, u32[]{:S(2)}) collective-permute-start(bf16[512,128]{1,0:T(8,128)(2,1)S(1)} %get-tuple-element.47), channel_id=1, source_target_pairs={{0,192},{1,193},{2,194},{3,195},{4,196},{5,197},{6,198},{7,199},{8... | collective-permute-start | bytes 393224 | tf_op jit(solution)/shard_map/ppermute | solution.py:32
  60.0 25.4 %collective-permute-start.12 = (f32[4,128,512]{2,1,0:T(8,128)S(1)}, f32[4,128,512]{2,1,0:T(8,128)S(1)}, u32[]{:S(2)}, u32[]{:S(2)}) collective-permute-start(f32[4,128,512]{2,1,0:T(8,128)S(1)} %get-tuple-element.38), channel_id=1, source_target_pairs={{0,1},{1,0},{2,3},{3,2},{4,5},{5,4},{6,7},{7,6},{8,9},{9,8},{10,11... | collective-permute-start | bytes 3145736 | tf_op jit(solution)/shard_map/ppermute | solution.py:32
  75.4 9.8 %collective-permute-start.27 = (bf16[128,1024]{1,0:T(8,128)(2,1)S(1)}, bf16[128,1024]{1,0:T(8,128)(2,1)S(1)}, u32[]{:S(2)}, u32[]{:S(2)}) collective-permute-start(bf16[128,1024]{1,0:T(8,128)(2,1)S(1)} %get-tuple-element.59), channel_id=1, source_target_pairs={{0,4},{1,5},{2,6},{3,7},{4,8},{5,9},{6,10},{7,11},{8,12},{9,13},{1... | collective-permute-start | bytes 786440 | tf_op jit(solution)/shard_map/ppermute | solution.py:32
  75.6 16.1 %collective-permute-start.28 = (bf16[128,1024]{1,0:T(8,128)(2,1)S(1)}, bf16[128,1024]{1,0:T(8,128)(2,1)S(1)}, u32[]{:S(2)}, u32[]{:S(2)}) collective-permute-start(bf16[128,1024]{1,0:T(8,128)(2,1)S(1)} %get-tuple-element.60), channel_id=1, source_target_pairs={{0,8},{1,9},{2,10},{3,11},{4,12},{5,13},{6,14},{7,15},{8,0},{9,1},... | collective-permute-start | bytes 786440 | tf_op jit(solution)/shard_map/ppermute | solution.py:32
  80.1 21.0 %collective-permute-start.29 = (bf16[128,1024]{1,0:T(8,128)(2,1)S(1)}, bf16[128,1024]{1,0:T(8,128)(2,1)S(1)}, u32[]{:S(2)}, u32[]{:S(2)}) collective-permute-start(bf16[128,1024]{1,0:T(8,128)(2,1)S(1)} %get-tuple-element.61), channel_id=1, source_target_pairs={{0,12},{1,13},{2,14},{3,15},{4,0},{5,1},{6,2},{7,3},{8,4},{9,5},{1... | collective-permute-start | bytes 786440 | tf_op jit(solution)/shard_map/ppermute | solution.py:32
  82.0 22.0 %collective-permute-start.21 = (bf16[128,1024]{1,0:T(8,128)(2,1)S(1)}, bf16[128,1024]{1,0:T(8,128)(2,1)S(1)}, u32[]{:S(2)}, u32[]{:S(2)}) collective-permute-start(bf16[128,1024]{1,0:T(8,128)(2,1)S(1)} %get-tuple-element.50), channel_id=1, source_target_pairs={{0,4},{1,5},{2,6},{3,7},{4,8},{5,9},{6,10},{7,11},{8,12},{9,13},{1... | collective-permute-start | bytes 786440 | tf_op jit(solution)/shard_map/ppermute | solution.py:32
  85.2 18.8 %collective-permute-start.22 = (bf16[128,1024]{1,0:T(8,128)(2,1)S(1)}, bf16[128,1024]{1,0:T(8,128)(2,1)S(1)}, u32[]{:S(2)}, u32[]{:S(2)}) collective-permute-start(bf16[128,1024]{1,0:T(8,128)(2,1)S(1)} %get-tuple-element.51), channel_id=1, source_target_pairs={{0,8},{1,9},{2,10},{3,11},{4,12},{5,13},{6,14},{7,15},{8,0},{9,1},... | collective-permute-start | bytes 786440 | tf_op jit(solution)/shard_map/ppermute | solution.py:32
  85.4 19.9 %collective-permute-start.23 = (bf16[128,1024]{1,0:T(8,128)(2,1)S(1)}, bf16[128,1024]{1,0:T(8,128)(2,1)S(1)}, u32[]{:S(2)}, u32[]{:S(2)}) collective-permute-start(bf16[128,1024]{1,0:T(8,128)(2,1)S(1)} %get-tuple-element.52), channel_id=1, source_target_pairs={{0,12},{1,13},{2,14},{3,15},{4,0},{5,1},{6,2},{7,3},{8,4},{9,5},{1... | collective-permute-start | bytes 786440 | tf_op jit(solution)/shard_map/ppermute | solution.py:32
  91.7 24.5 %collective-permute-start.13 = (bf16[4,64,512]{2,1,0:T(8,128)(2,1)S(1)}, bf16[4,64,512]{2,1,0:T(8,128)(2,1)S(1)}, u32[]{:S(2)}, u32[]{:S(2)}) collective-permute-start(bf16[4,64,512]{2,1,0:T(8,128)(2,1)S(1)} %get-tuple-element.40), channel_id=1, source_target_pairs={{0,2},{1,3},{2,0},{3,1},{4,6},{5,7},{6,4},{7,5},{8,10},{9,11},{10,... | collective-permute-start | bytes 786440 | tf_op jit(solution)/shard_map/ppermute | solution.py:32
  101.8 16.2 %collective-permute-start.30 = (bf16[32,1152]{1,0:T(8,128)(2,1)S(1)}, bf16[32,1152]{1,0:T(8,128)(2,1)S(1)}, u32[]{:S(2)}, u32[]{:S(2)}) collective-permute-start(bf16[32,1152]{1,0:T(8,128)(2,1)S(1)} %get-tuple-element.64), channel_id=1, source_target_pairs={{0,16},{1,17},{2,18},{3,19},{4,20},{5,21},{6,22},{7,23},{8,24},{9,... | collective-permute-start | bytes 221192 | tf_op jit(solution)/shard_map/ppermute | solution.py:32
  104.0 14.3 %collective-permute-start.31 = (bf16[32,1152]{1,0:T(8,128)(2,1)S(1)}, bf16[32,1152]{1,0:T(8,128)(2,1)S(1)}, u32[]{:S(2)}, u32[]{:S(2)}) collective-permute-start(bf16[32,1152]{1,0:T(8,128)(2,1)S(1)} %get-tuple-element.65), channel_id=1, source_target_pairs={{0,32},{1,33},{2,34},{3,35},{4,36},{5,37},{6,38},{7,39},{8,40},{9,... | collective-permute-start | bytes 221192 | tf_op jit(solution)/shard_map/ppermute | solution.py:32
  104.0 17.3 %collective-permute-start.32 = (bf16[32,1152]{1,0:T(8,128)(2,1)S(1)}, bf16[32,1152]{1,0:T(8,128)(2,1)S(1)}, u32[]{:S(2)}, u32[]{:S(2)}) collective-permute-start(bf16[32,1152]{1,0:T(8,128)(2,1)S(1)} %get-tuple-element.66), channel_id=1, source_target_pairs={{0,48},{1,49},{2,50},{3,51},{4,52},{5,53},{6,54},{7,55},{8,56},{9,... | collective-permute-start | bytes 221192 | tf_op jit(solution)/shard_map/ppermute | solution.py:32
  106.1 15.2 %collective-permute-start.24 = (bf16[32,1152]{1,0:T(8,128)(2,1)S(1)}, bf16[32,1152]{1,0:T(8,128)(2,1)S(1)}, u32[]{:S(2)}, u32[]{:S(2)}) collective-permute-start(bf16[32,1152]{1,0:T(8,128)(2,1)S(1)} %get-tuple-element.55), channel_id=1, source_target_pairs={{0,16},{1,17},{2,18},{3,19},{4,20},{5,21},{6,22},{7,23},{8,24},{9,... | collective-permute-start | bytes 221192 | tf_op jit(solution)/shard_map/ppermute | solution.py:32
  116.8 11.3 %collective-permute-start.14 = (f32[64,512]{1,0:T(8,128)S(1)}, f32[64,512]{1,0:T(8,128)S(1)}, u32[]{:S(2)}, u32[]{:S(2)}) collective-permute-start(f32[64,512]{1,0:T(8,128)S(1)} %get-tuple-element.42), channel_id=1, source_target_pairs={{0,192},{1,193},{2,194},{3,195},{4,196},{5,197},{6,198},{7,199},{8... | collective-permute-start | bytes 393224 | tf_op jit(solution)/shard_map/ppermute | solution.py:32
  118.0 10.1 %collective-permute-start.15 = (f32[64,512]{1,0:T(8,128)S(1)}, f32[64,512]{1,0:T(8,128)S(1)}, u32[]{:S(2)}, u32[]{:S(2)}) collective-permute-start(f32[64,512]{1,0:T(8,128)S(1)} %get-tuple-element.43), channel_id=1, source_target_pairs={{0,128},{1,129},{2,130},{3,131},{4,132},{5,133},{6,134},{7,135},{8... | collective-permute-start | bytes 393224 | tf_op jit(solution)/shard_map/ppermute | solution.py:32
  118.3 9.9 %collective-permute-start.16 = (f32[64,512]{1,0:T(8,128)S(1)}, f32[64,512]{1,0:T(8,128)S(1)}, u32[]{:S(2)}, u32[]{:S(2)}) collective-permute-start(f32[64,512]{1,0:T(8,128)S(1)} %get-tuple-element.44), channel_id=1, source_target_pairs={{0,64},{1,65},{2,66},{3,67},{4,68},{5,69},{6,70},{7,71},{8,72},{9,... | collective-permute-start | bytes 393224 | tf_op jit(solution)/shard_map/ppermute | solution.py:32
  121.2 5.6 %collective-permute-start.26 = (bf16[32,1152]{1,0:T(8,128)(2,1)S(1)}, bf16[32,1152]{1,0:T(8,128)(2,1)S(1)}, u32[]{:S(2)}, u32[]{:S(2)}) collective-permute-start(bf16[32,1152]{1,0:T(8,128)(2,1)S(1)} %get-tuple-element.57), channel_id=1, source_target_pairs={{0,48},{1,49},{2,50},{3,51},{4,52},{5,53},{6,54},{7,55},{8,56},{9,... | collective-permute-start | bytes 221192 | tf_op jit(solution)/shard_map/ppermute | solution.py:32
  129.1 17.0 %collective-permute-start.33 = (bf16[64,2176]{1,0:T(8,128)(2,1)S(1)}, bf16[64,2176]{1,0:T(8,128)(2,1)S(1)}, u32[]{:S(2)}, u32[]{:S(2)}) collective-permute-start(bf16[64,2176]{1,0:T(8,128)(2,1)S(1)} %shard_map.95.own), channel_id=1, source_target_pairs={{0,2},{1,3},{2,0},{3,1},{4,6},{5,7},{6,4},{7,5},{8,10},{9,11},{10,... | collective-permute-start | bytes 835592 | tf_op jit(solution)/shard_map/ppermute | solution.py:32
  133.1 15.1 %collective-permute-start.34 = (bf16[64,2176]{1,0:T(8,128)(2,1)S(1)}, bf16[64,2176]{1,0:T(8,128)(2,1)S(1)}, u32[]{:S(2)}, u32[]{:S(2)}) collective-permute-start(bf16[64,2176]{1,0:T(8,128)(2,1)S(1)} %shard_map.95.own), channel_id=1, source_target_pairs={{0,1},{1,0},{2,3},{3,2},{4,5},{5,4},{6,7},{7,6},{8,9},{9,8},{10,11... | collective-permute-start | bytes 835592 | tf_op jit(solution)/shard_map/ppermute | solution.py:32
  (13 other events, 115.0 us)
